TPU v7x, 256 devices: a whole 4x4x8 slice. The times are simulated.
256 devices in a mesh: seq: 32 (over z, x_hi, core), tp: 8 (over x_lo, y).
Axes of the slice: x: 4 (x_hi: 2, x_lo: 2; x = x_hi * 2 + x_lo), y: 4, z: 8, core: 2. Of those that a mesh axis runs over, the one named last changes fastest.
Arguments:
- tokens: bfloat16 [8192, 2048], P('seq', 'tp'), may hold values from -6 to 6
- ctx_len: int32 [32], P('seq'), may hold values from 0 to 12288, as said below
- cache_kv: bfloat16 [32, 4096, 2, 2048], P('seq', None, None, 'tp'), may hold values from -80 to 80, as said below
- cache_pos: int32 [32, 4096], P('seq'), may hold values from -1 to 12287, as said below
- attn_gain: float32 [2048], replicated, may hold values from 0.5 to 1.5
- moe_gain: float32 [2048], replicated, may hold values from 0.5 to 1.5
- qkv_train: float32 [2048, 3, 2048], P('seq', None, 'tp'), may hold values from -0.125 to 0.125
- out_train: float32 [2048, 2048], P('seq', 'tp'), may hold values from -0.125 to 0.125
- router: bfloat16 [2048, 64], replicated, may hold values from -0.125 to 0.125
- routes: int32 [8192, 6], P('seq'), may hold values from 0 to 63, all different within a row; in each aligned block of 256 rows (0 to 255, 256 to 511, ...) at most 32 rows name the same one
- handed_half: int32 [32], replicated, may hold values from 0 to 1
- fresh_gu: float32 [32, 1408, 2, 2048], P('seq', 'tp'), may hold values from -0.125 to 0.125
- fresh_down: float32 [32, 1408, 2048], P('seq', 'tp'), may hold values from -0.15625 to 0.15625
- server_gu: bfloat16 [32, 2816, 2, 2048], P('seq', 'tp'), may hold values from -0.125 to 0.125
- server_down: bfloat16 [32, 2816, 2048], P('seq', 'tp'), may hold values from -0.15625 to 0.15625
Outputs:
- layer_out: bfloat16 [8192, 2048], P('seq', 'tp')
Inputs may be any that keep to these rules, and one draw needn't show every extreme that they name: `ctx_len`: some request has exactly 12288 cached positions and some has none. `cache_pos`: -1 marks an empty slot. With a context length L of at most 4096, slot s holds position s for s < L. With a longer context, slots below 4 hold positions 0 to 3 and the other slots hold positions L - 4092 to L - 1, each once. `routes`: each row names 6 different experts; in the rows of one request no expert is named by more than 32 rows, and in every draw some expert by exactly 32. `cache_kv`: keys already carry their position's rotation.
All inputs are finite; a program needn't handle non-finite values.
Results may differ from a plain program's by a relative error of at most 0.025.
Values may be sent and summed in bfloat16 or wider, within the bound.
A program may use at most 128 MiB of HBM per device.

v0:
```python
import jax
import jax.numpy as jnp
from jax import lax
from jax.sharding import PartitionSpec as P

HEAD_DIM = 128
SINK = 4
WIN = 4096


def swapped(array, axis, apart):
    return lax.ppermute(array, axis, [(i, i ^ 1 << apart) for i in range(lax.axis_size(axis))])


def normed(field, gain_vec):
    values_in = field.astype(jnp.float32)
    inv_rms = lax.rsqrt(jnp.mean(values_in * values_in, axis=-1, keepdims=True) + 1e-06)
    return (values_in * inv_rms * gain_vec).astype(jnp.bfloat16)


def rotate(field, positions):
    half_dim = field.shape[-1] // 2
    frequency = 10000.0 ** (-jnp.arange(half_dim, dtype=jnp.float32) / half_dim)
    angles = positions.astype(jnp.float32)[:, None] * frequency[None, :]
    cosine = jnp.cos(angles)[:, None, :]
    sine = jnp.sin(angles)[:, None, :]
    first_half = field[..., :half_dim]
    second_half = field[..., half_dim:]
    return jnp.concatenate(
        [first_half * cosine - second_half * sine, second_half * cosine + first_half * sine],
        axis=-1,
    )


def attend(queries, keys_new, values_new, cache_keys, cache_values, slot_pos, context):
    new_count = queries.shape[0]
    key_all = jnp.concatenate([cache_keys, keys_new], axis=0)
    value_all = jnp.concatenate([cache_values, values_new], axis=0)
    scores = jnp.einsum(
        "qhd,khd->hqk", queries, key_all, preferred_element_type=jnp.float32
    ) / jnp.sqrt(jnp.float32(HEAD_DIM))
    token_ids = jnp.arange(new_count, dtype=jnp.int32)
    positions = context + token_ids
    cache_ok = (slot_pos[None, :] >= 0) & (
        (slot_pos[None, :] < SINK) | (positions[:, None] - slot_pos[None, :] < WIN)
    )
    new_ok = token_ids[None, :] <= token_ids[:, None]
    allowed = jnp.concatenate([cache_ok, new_ok], axis=1)
    scores = jnp.where(allowed[None], scores, jnp.float32(-1e30))
    row_top = jnp.max(scores, axis=-1, keepdims=True)
    weights = jnp.exp(scores - row_top)
    row_total = jnp.sum(weights, axis=-1, keepdims=True)
    probability = (weights / row_total).astype(jnp.bfloat16)
    return jnp.einsum(
        "hqk,khd->qhd", probability, value_all, preferred_element_type=jnp.float32
    ).astype(jnp.bfloat16)


def body(
    tokens,
    ctx_len,
    cache_kv,
    cache_pos,
    attn_gain,
    moe_gain,
    qkv_train,
    out_train,
    router,
    routes,
    handed_half,
    fresh_gu,
    fresh_down,
    server_gu,
    server_down,
):
    seq_count = lax.axis_size("seq")
    tp_place = lax.axis_index("tp")
    seq_place = lax.axis_index("seq")
    full_tokens = lax.all_gather(tokens, "tp", axis=1, tiled=True)
    tok_rows = full_tokens.shape[0]
    model_width = full_tokens.shape[1]
    qkv_all, out_all = (
        lax.all_gather(qkv_train.astype(jnp.bfloat16), "seq", axis=0, tiled=True),
        lax.all_gather(out_train.astype(jnp.bfloat16), "seq", axis=0, tiled=True),
    )
    local_width = qkv_all.shape[2]
    heads_here = local_width // HEAD_DIM
    normed_x = normed(full_tokens, attn_gain)
    projected = jnp.dot(
        normed_x, qkv_all.reshape(model_width, 3 * local_width), preferred_element_type=jnp.float32
    )
    projected = projected.reshape(tok_rows, 3, heads_here, HEAD_DIM)
    context = ctx_len[0]
    positions = context + jnp.arange(tok_rows, dtype=jnp.int32)
    queries = rotate(projected[:, 0], positions).astype(jnp.bfloat16)
    keys_new = rotate(projected[:, 1], positions).astype(jnp.bfloat16)
    values_new = projected[:, 2].astype(jnp.bfloat16)
    slot_count = cache_kv.shape[1]
    cached = cache_kv[0].reshape(slot_count, 2, heads_here, HEAD_DIM)
    mixed_heads = attend(
        queries, keys_new, values_new, cached[:, 0], cached[:, 1], cache_pos[0], context
    )
    mixed_heads = mixed_heads.reshape(tok_rows, local_width)
    partial_out = lax.dot_general(
        mixed_heads, out_all, (((1,), (1,)), ((), ())), preferred_element_type=jnp.float32
    )
    attn_total = lax.psum(partial_out.astype(jnp.bfloat16), "tp").astype(jnp.float32)
    hidden_state = (full_tokens.astype(jnp.float32) + attn_total).astype(jnp.bfloat16)
    moe_in = normed(hidden_state, moe_gain)
    logits = jnp.dot(moe_in, router, preferred_element_type=jnp.float32)
    gate_values = jax.nn.sigmoid(jnp.take_along_axis(logits, routes, axis=1))
    expert_count = router.shape[1]
    top_count = routes.shape[1]
    capacity = tok_rows // 8
    flat_routes = routes.reshape(-1)
    onehot = (flat_routes[:, None] == jnp.arange(expert_count, dtype=jnp.int32)[None, :]).astype(
        jnp.int32
    )
    before = jnp.cumsum(onehot, axis=0) - onehot
    slot_rank = jnp.sum(before * onehot, axis=1)
    slot_index = flat_routes * capacity + slot_rank
    repeated = jnp.repeat(moe_in, top_count, axis=0)
    outgoing = (
        jnp.zeros((expert_count * capacity, model_width), jnp.bfloat16).at[slot_index].set(repeated)
    )
    per_device = expert_count // seq_count
    pair_count = per_device // 2
    outgoing = outgoing.reshape(seq_count, per_device, capacity, model_width)
    arrived = lax.all_to_all(outgoing, "seq", split_axis=0, concat_axis=0, tiled=True)
    parity = tp_place % 2
    own_gu = fresh_gu.astype(jnp.bfloat16)
    own_down = fresh_down.astype(jnp.bfloat16)
    other_gu, other_down = swapped((own_gu, own_down), "tp", 0)
    lower_first = parity == 0
    group_gu = jnp.where(
        lower_first,
        jnp.concatenate([own_gu, other_gu], axis=1),
        jnp.concatenate([other_gu, own_gu], axis=1),
    )
    group_down = jnp.where(
        lower_first,
        jnp.concatenate([own_down, other_down], axis=1),
        jnp.concatenate([other_down, own_down], axis=1),
    )
    local_half = lax.dynamic_slice_in_dim(handed_half, seq_place * pair_count, pair_count, 0)
    use_fresh = local_half == parity
    weights_gu = jnp.where(use_fresh[:, None, None, None], group_gu, server_gu)
    weights_down = jnp.where(use_fresh[:, None, None], group_down, server_down)
    arrived_pairs = arrived.reshape(seq_count, pair_count, 2, capacity, model_width)
    mine = lax.dynamic_index_in_dim(arrived_pairs, parity, 2, keepdims=False)
    pre_act = jnp.einsum("sqcd,qfgd->sqcgf", mine, weights_gu, preferred_element_type=jnp.float32)
    activated = (jax.nn.silu(pre_act[..., 0, :]) * pre_act[..., 1, :]).astype(jnp.bfloat16)
    partial_y = jnp.einsum(
        "sqcf,qfd->sqcd", activated, weights_down, preferred_element_type=jnp.float32
    )
    selector = (jnp.arange(2, dtype=jnp.int32) == parity).astype(jnp.float32)
    placed = partial_y[:, :, None] * selector[None, None, :, None, None]
    placed = placed.reshape(seq_count, per_device, capacity, model_width)
    summed = lax.psum_scatter(placed.astype(jnp.bfloat16), "tp", scatter_dimension=3, tiled=True)
    returned = lax.all_to_all(summed, "seq", split_axis=0, concat_axis=0, tiled=True)
    part_width = returned.shape[3]
    flat_back = returned.reshape(expert_count * capacity, part_width)
    picked = flat_back[slot_index].reshape(tok_rows, top_count, part_width)
    combined = jnp.sum(gate_values[:, :, None] * picked.astype(jnp.float32), axis=1)
    residual = lax.dynamic_slice_in_dim(hidden_state, tp_place * part_width, part_width, 1)
    return (residual.astype(jnp.float32) + combined).astype(jnp.bfloat16)


def solution(mesh):
    placed = (
        P("seq", "tp"),
        P("seq"),
        P("seq", None, None, "tp"),
        P("seq", None),
        P(),
        P(),
        P("seq", None, "tp"),
        P("seq", "tp"),
        P(),
        P("seq", None),
        P(),
        P("seq", "tp", None, None),
        P("seq", "tp", None),
        P("seq", "tp", None, None),
        P("seq", "tp", None),
    )
    return jax.shard_map(
        body, mesh=mesh, in_specs=placed, out_specs=P("seq", "tp"), check_vma=False
    )
```

profile of v0, /device:TPU:1, one launch (start us, length us, event | category | flops | bytes accessed | tf_op | source)
XLA Modules:
  0.0 695.0 jit_solution(49394141733792327)
XLA Ops:
  12.0 11.2 %copy.54 = bf16[1,4096,2,256]{1,3,2,0:T(8,128)(2,1)} copy(bf16[1,4096,2,256]{3,2,1,0:T(2,128)(2,1)} %param.17) | data formatting | bytes 8388608 | tf_op args[2]
  23.2 4.0 slice_bitcast_fusion
  27.2 2.4 copy.73
  31.1 17.8 %all-gather.4.cloned.1.call-done = bf16[256,2048]{1,0:T(8,128)(2,1)} async-done(((bf16[256,256]{1,0:T(8,128)(2,1)}), bf16[256,2048]{1,0:T(8,128)(2,1)}) %all-gather.4.cloned.1.call-update) | async-done | bytes 1048592 | tf_op jit(solution)/shard_map/all_gather | solution.py:79
  50.5 90.5 %all-gather.6.cloned.1.call-done = bf16[2048,3,256]{2,0,1:T(8,128)(2,1)} async-done(((bf16[64,3,256]{2,0,1:T(8,128)(2,1)}), bf16[2048,3,256]{2,0,1:T(8,128)(2,1)}) %all-gather.6.cloned.1.call-update) | async-done | bytes 3145744 | tf_op jit(solution)/shard_map/all_gather | solution.py:83
  140.9 4.7 copy.55
  145.6 3.0 fusion.45
  149.6 5.3 multiply_select_fusion
  155.9 2.3 exponential_reduce_fusion
  158.2 3.4 fusion.41
  161.6 56.5 %all-gather.8.cloned.1.call-done = bf16[2048,256]{1,0:T(8,128)(2,1)} async-done(((bf16[64,256]{1,0:T(8,128)(2,1)}), bf16[2048,256]{1,0:T(8,128)(2,1)}) %all-gather.8.cloned.1.call-update) | async-done | bytes 1048592 | tf_op jit(solution)/shard_map/all_gather | solution.py:84
  218.1 2.7 convolution_convert_fusion
  221.3 18.3 %reduce-window.6 = s32[64,12,128]{2,1,0:T(8,128)S(1)} reduce-window(s32[64,12,128]{2,1,0:T(8,128)S(1)} %fusion.51, s32[]{:T(128)} %constant.29.clone.1), window={size=1x1x128 pad=0_0x0_0x127_0}, to_apply=%region_5.6 | reduce-window | flops 12484608 | bytes 786436 | tf_op jit(solution)/shard_map/reduce-window
  241.0 53.8 %all-reduce.2.cloned.1.call-done = bf16[256,2048]{1,0:T(8,128)(2,1)} async-done(((bf16[256,2048]{1,0:T(8,128)(2,1)}), bf16[256,2048]{1,0:T(8,128)(2,1)}) %all-reduce.2.cloned.1.call-update) | async-done | bytes 1048592 | tf_op jit(solution)/shard_map/psum | solution.py:107
  294.8 1.7 fusion.18
  297.8 4.6 broadcast_in_dim.42
  302.4 11.1 %reshape.346 = bf16[1536,2048]{1,0:T(8,128)(2,1)} reshape(bf16[256,6,2048]{2,1,0:T(8,128)(2,1)} %broadcast_in_dim.42) | data formatting | bytes 12582912 | tf_op jit(solution)/shard_map/reshape | solution.py:122
  313.5 15.1 %scatter_custom_fusion = bf16[2048,2048]{1,0:T(8,128)(2,1)} fusion(s32[1536]{0:T(1024)S(1)} %fusion.59, bf16[1536,2048]{1,0:T(8,128)(2,1)} %reshape.346, bf16[]{:T(256)} %constant.85.clone.1), kind=kCustom, calls=%fused_computation.17 | custom fusion | bytes 8389120 | tf_op jit(solution)/shard_map/scatter | solution.py:124
  328.5 15.0 %all-to-all-start = ((bf16[32,2,32,2048]{3,2,1,0:T(8,128)(2,1)}), bf16[32,2,32,2048]{3,2,1,0:T(8,128)(2,1)}, u32[]{:S(2)}, u32[]{:S(2)}) async-start(bf16[32,2,32,2048]{3,2,1,0:T(8,128)(2,1)} %bitcast.87), calls=%async_computation | async-start | bytes 16777216 | tf_op jit(solution)/shard_map/all_to_all | solution.py:129
  343.9 3.3 convert_element_type.111
  350.0 30.2 %collective-permute-done.1 = bf16[1,176,2,2048]{3,2,1,0:T(2,128)(2,1)} collective-permute-done((bf16[1,176,2,2048]{3,2,1,0:T(2,128)(2,1)S(1)}, bf16[1,176,2,2048]{3,2,1,0:T(2,128)(2,1)}, u32[]{:S(2)}, u32[]{:S(2)}) %collective-permute-start.1) | collective-permute-done | bytes 1441824 | tf_op jit(solution)/shard_map/ppermute | solution.py:12
  380.2 16.0 %fusion.10 = bf16[352,2,2048,1]{2,1,0,3:T(2,128)(2,1)} fusion(bf16[1,352,2,2048]{3,2,1,0:T(2,128)(2,1)} %param.28, pred[]{:T(512)} %bitcast.17, pred[]{:T(512)S(6)} %eq.48, bf16[1,176,2,2048]{3,2,1,0:T(2,128)(2,1)} %collective-permute-done.1, bf16[1,176,2,2048]{3,2,1,0:T(2,128)(2,1)S(1)} %convert_element_type.111), kind=kLoop, calls=%fused_computation.25 | loop fusion | flops 5767168 | bytes 8650754 | tf_op jit(solution)/shard_map/reshape.10
  396.2 133.9 %all-to-all-done = bf16[32,2,32,2048]{3,2,1,0:T(8,128)(2,1)} async-done(((bf16[32,2,32,2048]{3,2,1,0:T(8,128)(2,1)}), bf16[32,2,32,2048]{3,2,1,0:T(8,128)(2,1)}, u32[]{:S(2)}, u32[]{:S(2)}) %all-to-all-start) | async-done | bytes 8388640 | tf_op jit(solution)/shard_map/all_to_all | solution.py:129
  530.1 7.3 %fusion.25 = f32[32,1,32,2,352]{4,2,0,3,1:T(8,128)S(1)} fusion(bf16[32,2,32,2048]{3,2,1,0:T(8,128)(2,1)} %all-to-all-done, s32[]{:T(128)S(6)} %select_n.95, bf16[352,2,2048,1]{2,1,0,3:T(2,128)(2,1)} %fusion.10), kind=kOutput, calls=%fused_computation.45 | convolution fusion | flops 2952790016 | bytes 9961476 | tf_op jit(solution)/shard_map/sqcd,qfgd->sqcgf/dot_general | solution.py:151
  537.4 7.0 %convolution_bitcast_fusion = f32[32,32,2048]{2,1,0:T(8,128)} fusion(bf16[1,352,2048]{2,1,0:T(8,128)(2,1)S(1)} %copy-done.8, bf16[1,176,2048]{2,1,0:T(8,128)(2,1)} %collective-permute-done, bf16[1,176,2048]{2,1,0:T(8,128)(2,1)S(1)} %convert_element_type.110, pred[]{:T(512)S(6)} %eq.48, pred[]{:T(512)} %bitcast.17, f32[32,1,32,2,352]{4,2,0,3,1:T(8,128)S(1)} %fusion.25), kind=kOutput, calls=%fused_computation.13 | convolution fusion | flops 1485766656 | bytes 14155778 | tf_op jit(solution)/shard_map/sqcf,qfd->sqcd/dot_general | solution.py:153
  544.5 8.5 %multiply_convert_fusion = bf16[32,2,32,2048]{3,2,1,0:T(8,128)(2,1)} fusion(f32[2]{0:T(128)S(1)} %compare_convert_fusion, f32[32,32,2048]{2,1,0:T(8,128)} %convolution_bitcast_fusion), kind=kLoop, calls=%fused_computation.4 | loop fusion | flops 8388608 | bytes 16777224 | tf_op jit(solution)/shard_map/convert_element_type | solution.py:159
  553.0 90.4 %reduce-scatter.2.cloned.1.call-done = bf16[32,2,32,256]{3,2,1,0:T(8,128)(2,1)} async-done(((bf16[32,2,32,2048]{3,2,1,0:T(8,128)(2,1)}), bf16[32,2,32,256]{3,2,1,0:T(8,128)(2,1)}) %reduce-scatter.2.cloned.1.call-update) | async-done | bytes 1048592 | tf_op jit(solution)/shard_map/reduce_scatter | solution.py:159
  643.4 9.9 %all-to-all-start.1 = ((bf16[32,2,32,256]{3,2,1,0:T(8,128)(2,1)}), bf16[32,2,32,256]{3,2,1,0:T(8,128)(2,1)S(1)}, u32[]{:S(2)}, u32[]{:S(2)}) async-start(bf16[32,2,32,256]{3,2,1,0:T(8,128)(2,1)} %reduce-scatter.2.cloned.1.call-done), calls=%async_computation.2 | async-start | bytes 2097152 | tf_op jit(solution)/shard_map/all_to_all | solution.py:160
  654.1 12.7 %gather_fusion.1 = f32[1536]{0:T(1024)S(1)} fusion(f32[256,64]{0,1:T(8,128)S(1)} %fusion.67, s32[1536]{0:T(1024)S(1)} %reshape.336), kind=kCustom, calls=%fused_computation.1 | custom fusion | bytes 24576 | tf_op jit(solution)/shard_map/jit(take_along_axis)/gather | solution.py:111
  667.2 14.0 %all-to-all-done.1 = bf16[32,2,32,256]{3,2,1,0:T(8,128)(2,1)S(1)} async-done(((bf16[32,2,32,256]{3,2,1,0:T(8,128)(2,1)}), bf16[32,2,32,256]{3,2,1,0:T(8,128)(2,1)S(1)}, u32[]{:S(2)}, u32[]{:S(2)}) %all-to-all-start.1) | async-done | bytes 1048608 | tf_op jit(solution)/shard_map/all_to_all | solution.py:160
  681.2 4.8 gather_fusion
  686.9 1.6 add_convert_fusion
  (81 shorter events, 17.3 us)
Async XLA Ops:
  6.5 647.1 %copy-start = (bf16[2048,64]{0,1:T(8,128)(2,1)S(1)}, bf16[2048,64]{0,1:T(8,128)(2,1)}, u32[]{:S(2)}) copy-start(bf16[2048,64]{0,1:T(8,128)(2,1)} %param.23) | copy-start | bytes 786436
  6.5 42.4 %all-gather.4.cloned.1.call-start = ((), (), s32[]{:S(2)}) async-start(), calls=%async_computation.3 | async-start | bytes 1179648 | tf_op jit(solution)/shard_map/all_gather | solution.py:79
  7.3 133.7 %all-gather.6.cloned.1.call-start = ((), (), s32[]{:S(2)}) async-start(), calls=%async_computation.4 | async-start | bytes 3244032 | tf_op jit(solution)/shard_map/all_gather | solution.py:83
  8.9 209.2 %all-gather.8.cloned.1.call-start = ((), (), s32[]{:S(2)}) async-start(), calls=%async_computation.5 | async-start | bytes 1081344 | tf_op jit(solution)/shard_map/all_gather | solution.py:84
  10.4 284.3 %all-reduce.2.cloned.1.call-start = ((), (), s32[]{:S(2)}) async-start(), calls=%async_computation.6 | async-start | bytes 2097152 | tf_op jit(solution)/shard_map/psum | solution.py:107
  27.2 2.8 copy-start.6
  50.5 95.2 %copy-start.2 = (bf16[256,2048]{1,0:T(8,128)(2,1)S(1)}, bf16[256,2048]{1,0:T(8,128)(2,1)}, u32[]{:S(2)}) copy-start(bf16[256,2048]{1,0:T(8,128)(2,1)} %all-gather.4.cloned.1.call-done) | copy-start | bytes 3145732
  50.5 95.2 %copy-start.9 = (f32[2048]{0:T(1024)S(1)}, f32[2048]{0:T(1024)}, u32[]{:S(2)}) copy-start(f32[2048]{0:T(1024)} %param.19) | copy-start | bytes 24580
  148.6 0.9 copy-start.4
  161.6 59.3 %copy-start.5 = (s32[256,6]{0,1:T(8,128)S(1)}, s32[256,6]{0,1:T(8,128)}, u32[]{:S(2)}) copy-start(s32[256,6]{0,1:T(8,128)} %param.24) | copy-start | bytes 18436
  239.9 57.6 %copy-start.7 = (f32[2048]{0:T(1024)S(1)}, f32[2048]{0:T(1024)}, u32[]{:S(2)}) copy-start(f32[2048]{0:T(1024)} %param.20) | copy-start | bytes 24580
  296.5 1.0 copy-start.1
  328.5 201.6 %all-to-all-start = ((bf16[32,2,32,2048]{3,2,1,0:T(8,128)(2,1)}), bf16[32,2,32,2048]{3,2,1,0:T(8,128)(2,1)}, u32[]{:S(2)}, u32[]{:S(2)}) async-start(bf16[32,2,32,2048]{3,2,1,0:T(8,128)(2,1)} %bitcast.87), calls=%async_computation | async-start | bytes 16777216 | tf_op jit(solution)/shard_map/all_to_all | solution.py:129
  343.6 5.3 copy-start.10
  343.6 299.8 %reduce-scatter.2.cloned.1.call-start = ((), (), s32[]{:S(2)}) async-start(), calls=%async_computation.7 | async-start | bytes 9437184 | tf_op jit(solution)/shard_map/reduce_scatter | solution.py:159
  343.9 3.4 copy-start.3
  347.1 33.1 %collective-permute-start.1 = (bf16[1,176,2,2048]{3,2,1,0:T(2,128)(2,1)S(1)}, bf16[1,176,2,2048]{3,2,1,0:T(2,128)(2,1)}, u32[]{:S(2)}, u32[]{:S(2)}) collective-permute-start(bf16[1,176,2,2048]{3,2,1,0:T(2,128)(2,1)S(1)} %convert_element_type.111), channel_id=1, source_target_pairs={{0,1},{1,0},{2,3},{3,2},{4,5},{5,4},{6,7},{7,6},{8,9},{9,8},{10,11... | collective-permute-start | bytes 4325384 | tf_op jit(solution)/shard_map/ppermute | solution.py:12
  347.4 190.1 %collective-permute-start = (bf16[1,176,2048]{2,1,0:T(8,128)(2,1)S(1)}, bf16[1,176,2048]{2,1,0:T(8,128)(2,1)}, u32[]{:S(2)}, u32[]{:S(2)}) collective-permute-start(bf16[1,176,2048]{2,1,0:T(8,128)(2,1)S(1)} %convert_element_type.110), channel_id=1, source_target_pairs={{0,1},{1,0},{2,3},{3,2},{4,5},{5,4},{6,7},{7,6},{8,9},{9,8},{10,11... | collective-permute-start | bytes 2162696 | tf_op jit(solution)/shard_map/ppermute | solution.py:12
  396.2 141.2 %copy-start.8 = (bf16[1,352,2048]{2,1,0:T(8,128)(2,1)S(1)}, bf16[1,352,2048]{2,1,0:T(8,128)(2,1)}, u32[]{:S(2)}) copy-start(bf16[1,352,2048]{2,1,0:T(8,128)(2,1)} %param.29) | copy-start | bytes 4325380
  643.4 37.8 %all-to-all-start.1 = ((bf16[32,2,32,256]{3,2,1,0:T(8,128)(2,1)}), bf16[32,2,32,256]{3,2,1,0:T(8,128)(2,1)S(1)}, u32[]{:S(2)}, u32[]{:S(2)}) async-start(bf16[32,2,32,256]{3,2,1,0:T(8,128)(2,1)} %reduce-scatter.2.cloned.1.call-done), calls=%async_computation.2 | async-start | bytes 2097152 | tf_op jit(solution)/shard_map/all_to_all | solution.py:160
Sparse Core Ops, SparseCore 0:
  9.1 39.8 all-gather.3
  51.7 89.1 all-gather.5
  143.7 74.3 all-gather.7
  221.0 73.7 all-reduce.1
  553.1 90.1 reduce-scatter.1
where the time goes:
time: 696 us; the launch traced here: 695 us
  waiting for transfers between devices  488 us (70%)
  local copies, waits for them, and re-layouts  76.1 us (11%)
  other arithmetic  60.2 us (9%)
  matrix products  29.1 us (4%)
  starting transfers between devices  27 us (4%)
  between operations  14.8 us (2%)
    all_to_all x1, waiting for transfers between devices, body(): lax.all_to_all(outgoing, 'seq', split_axis=0, concat_axis=0, tiled=True)  134 us
    all_gather x1, waiting for transfers between devices, body(): lax.all_gather(qkv_train.astype(jnp.bfloat16), 'seq', axis=0, tiled=True)  90.5 us
    reduce_scatter x1, waiting for transfers between devices, body(): lax.psum_scatter(placed.astype(jnp.bfloat16), 'tp', scatter_dimension=3,...  90.4 us
    all_gather x1, waiting for transfers between devices, body(): lax.all_gather(out_train.astype(jnp.bfloat16), 'seq', axis=0, tiled=True)  56.5 us
    psum x1, waiting for transfers between devices, body(): lax.psum(partial_out.astype(jnp.bfloat16), 'tp').astype(jnp.float32)  53.8 us
    another operation x5, other arithmetic  34.6 us
    ppermute x2, waiting for transfers between devices, swapped(): lax.ppermute(array, axis, [(i, i ^ 1 << apart) for i in range(lax.axis_si...  30.2 us
    all_gather x1, waiting for transfers between devices, body(): full_tokens = lax.all_gather(tokens, 'tp', axis=1, tiled=True)  17.8 us
  transfers between devices with their start and end apart: 9, of which 8 were waited for; matrix products, arithmetic and copies ran while one was open for 15% of the time, Pallas kernels for 0%

commit v1 on v0

v1 whole, which is shorter than its diff:
```python
import functools

import jax
import jax.numpy as jnp
from jax import lax
from jax.experimental import pallas as pl
from jax.experimental.pallas import tpu as pltpu
from jax.sharding import PartitionSpec as P

HEAD_DIM = 128
SINK = 4
WIN = 4096
MESH = pl.DeviceIdType.MESH
BF = jnp.bfloat16
F32 = jnp.float32
ANY = pl.BlockSpec(memory_space=pl.ANY)
VMEM = pl.BlockSpec(memory_space=pltpu.VMEM)
SMEM = pl.BlockSpec(memory_space=pltpu.SMEM)
DMA = pltpu.SemaphoreType.DMA
ORDER = (0, 1, 7, 2, 6, 3, 5, 4)


def places():
    return lax.axis_index("seq"), lax.axis_index("tp")


def greet(peers):
    barrier = pltpu.get_barrier_semaphore()
    for peer in peers:
        pl.semaphore_signal(barrier, inc=1, device_id=peer, device_id_type=MESH)
    pl.semaphore_wait(barrier, len(peers))


def push(src, dst, send, recv, peer):
    copy = pltpu.make_async_remote_copy(
        src_ref=src, dst_ref=dst, send_sem=send, recv_sem=recv, device_id=peer, device_id_type=MESH
    )
    copy.start()
    return copy


def tp_peers(s, t):
    return [(s, t ^ k) for k in range(1, 8)]


def seq_peer(s, t, k, j):
    z, r = s // 4, s % 4
    return ((z + k) % 8) * 4 + (r ^ j), t


def gather_kernel(tok, w, tok_all, w_all, lsem, tok_s, tok_r, x_s, x_r, z_s, z_r, c_s, c_r):
    s, t = places()
    z, xh, c = s // 4, (s // 2) % 2, s % 2
    up = (((z + 1) % 8) * 4 + xh * 2 + c, t)
    down = (((z + 7) % 8) * 4 + xh * 2 + c, t)
    over = (s ^ 2, t)
    twin = (s ^ 1, t)
    greet(tp_peers(s, t) + [up, down, over, twin])

    def block(dz, a):
        return w_all.at[(z + dz) % 8, xh ^ a, c]

    own = w.at[:, :]
    home = w_all.at[z, xh, c]
    waits = [push(own, home, x_s, x_r, over)]
    ups = {(0, 0): push(own, home, z_s.at[0, 0, 0], z_r.at[0, 0, 0], up)}
    downs = {(0, 0): push(own, home, z_s.at[1, 0, 0], z_r.at[1, 0, 0], down)}
    twins = [push(own, home, c_s.at[0, 0], c_r.at[0, 0], twin)]
    local_w = pltpu.make_async_copy(own, home, lsem.at[0])
    local_w.start()
    mine = tok_all.at[:, pl.ds(pl.multiple_of(t * 256, 256), 256)]
    local_t = pltpu.make_async_copy(tok, mine, lsem.at[1])
    local_t.start()
    toks = [push(tok, mine, tok_s.at[k], tok_r.at[k], (s, t ^ k)) for k in range(1, 8)]

    waits[0].wait_recv()
    theirs = block(0, 1)
    ups[(0, 1)] = push(theirs, theirs, z_s.at[0, 0, 1], z_r.at[0, 0, 1], up)
    downs[(0, 1)] = push(theirs, theirs, z_s.at[1, 0, 1], z_r.at[1, 0, 1], down)
    twins.append(push(theirs, theirs, c_s.at[0, 1], c_r.at[0, 1], twin))

    for step in range(4):
        for a in range(2):
            for way, (chain, peer, dz) in enumerate(((ups, up, -1 - step), (downs, down, 1 + step))):
                if (step, a) not in chain:
                    continue
                chain[(step, a)].wait_recv()
                here = block(dz + 8, a)
                if step < 2 or (step == 2 and a == way):
                    chain[(step + 1, a)] = push(
                        here, here, z_s.at[way, step + 1, a], z_r.at[way, step + 1, a], peer
                    )
                place = (dz + 8) % 8
                twins.append(push(here, here, c_s.at[place, a], c_r.at[place, a], twin))
    for copy in twins + toks:
        copy.wait()
    for copy in list(ups.values()) + list(downs.values()) + waits:
        copy.wait_send()
    local_w.wait()
    local_t.wait()


def gather(tok, w):
    return pl.pallas_call(
        gather_kernel,
        out_shape=(
            jax.ShapeDtypeStruct((256, 2048), BF),
            jax.ShapeDtypeStruct((8, 2, 2, 64, 1024), BF),
        ),
        in_specs=[ANY, ANY],
        out_specs=(ANY, ANY),
        scratch_shapes=[
            DMA((2,)),
            DMA((8,)),
            DMA((8,)),
            DMA,
            DMA,
            DMA((2, 4, 2)),
            DMA((2, 4, 2)),
            DMA((8, 2)),
            DMA((8, 2)),
        ],
        compiler_params=pltpu.CompilerParams(collective_id=0, has_side_effects=True),
        name="gather_inputs",
    )(tok, w)


def split_matrix(n):
    row = lax.broadcasted_iota(jnp.int32, (n, n), 0)
    col = lax.broadcasted_iota(jnp.int32, (n, n), 1)
    half = n // 2
    return jnp.where(col == jnp.where(row < half, 2 * row, 2 * (row - half) + 1), 1.0, 0.0).astype(BF)


def nt(a, b):
    return lax.dot_general(a, b, (((1,), (1,)), ((), ())), preferred_element_type=F32)


def attention_kernel(
    tok, w, gain, cosf, sinf, limit, cache, out, buf, vals, scores, top, total, acc, xn, sem
):
    chunks, width = 8, 512

    def fetch(i, h):
        rows = pl.ds(pl.multiple_of(i * width, width), width)
        return pltpu.make_async_copy(
            cache.at[rows, :, pl.ds(h * 128, 128)], buf.at[h, rows], sem.at[i, h]
        )

    for i in range(chunks):
        for h in range(2):
            fetch(i, h).start()
    field = tok[...].astype(F32)
    inv = lax.rsqrt(jnp.mean(field * field, axis=-1, keepdims=True) + 1e-6)
    xn[...] = (field * inv * gain[...]).astype(BF)
    projected = jnp.dot(xn[...], w[:, 0:768], preferred_element_type=F32)

    def turned(part):
        return (part * cosf[...] + pltpu.roll(part, 64, 1) * sinf[...]).astype(BF)

    queries = [turned(projected[:, h * 128 : h * 128 + 128]) for h in range(2)]
    keys_new = [turned(projected[:, 256 + h * 128 : 384 + h * 128]) for h in range(2)]
    values_new = [projected[:, 512 + h * 128 : 640 + h * 128].astype(BF) for h in range(2)]
    perm = split_matrix(256)
    row_id = lax.broadcasted_iota(jnp.int32, (256, width), 0)
    flat = [buf.at[h].reshape(8192, 128) for h in range(2)]

    new_row = lax.broadcasted_iota(jnp.int32, (256, 256), 0)
    new_col = lax.broadcasted_iota(jnp.int32, (256, 256), 1)
    for h in range(2):
        fresh = jnp.where(new_col <= new_row, nt(queries[h], keys_new[h]), -1e30)
        scores[h, chunks, :, 0:256] = fresh
        top[h] = jnp.maximum(fresh[:, 0:128], fresh[:, 128:256])

    @pl.loop(0, chunks)
    def _(i):
        for h in range(2):
            fetch(i, h).wait()
        keys = [[], []]
        for part in range(4):
            start = pl.multiple_of(i * 1024 + part * 256, 256)
            both = jnp.concatenate([flat[h][pl.ds(start, 256), :] for h in range(2)], axis=1)
            split = jnp.dot(perm, both, preferred_element_type=F32).astype(BF)
            spot = pl.multiple_of(i * width + part * 128, 128)
            vals[pl.ds(spot, 128), :] = split[128:256]
            for h in range(2):
                keys[h].append(split[0:128, h * 128 : h * 128 + 128])
        seen = row_id < limit[:, pl.ds(pl.multiple_of(i * width, width), width)]
        for h in range(2):
            key_block = jnp.concatenate(keys[h], axis=0)
            block = jnp.where(seen, nt(queries[h], key_block), -1e30)
            scores[h, i] = block
            peak = jnp.maximum(
                jnp.maximum(block[:, 0:128], block[:, 128:256]),
                jnp.maximum(block[:, 256:384], block[:, 384:512]),
            )
            top[h] = jnp.maximum(top[h], peak)

    scale = 1.4426950408889634 / (HEAD_DIM**0.5)
    for h in range(2):
        top[h] = jnp.broadcast_to(jnp.max(top[h], axis=1, keepdims=True), (256, 128))
        peak = top[h]
        weights = jnp.exp2((scores[h, chunks, :, 0:256] - jnp.tile(peak, (1, 2))) * scale)
        total[h] = weights[:, 0:128] + weights[:, 128:256]
        acc[h] = jnp.dot(weights.astype(BF), values_new[h], preferred_element_type=F32)

    @pl.loop(0, chunks)
    def _(i):
        for h in range(2):
            weights = jnp.exp2((scores[h, i] - jnp.tile(top[h], (1, 4))) * scale)
            total[h] += (weights[:, 0:128] + weights[:, 128:256]) + (
                weights[:, 256:384] + weights[:, 384:512]
            )
            spots = pl.ds(pl.multiple_of(i * width, width), width)
            acc[h] += jnp.dot(
                weights.astype(BF), vals[spots, h * 128 : h * 128 + 128], preferred_element_type=F32
            )

    mixed = jnp.concatenate(
        [(acc[h] / jnp.sum(total[h], axis=1, keepdims=True)).astype(BF) for h in range(2)], axis=1
    )
    for part in range(8):
        out[part] = nt(mixed, w[part * 256 : part * 256 + 256, 768:1024]).astype(BF)


def attention(tok, w, gain, cosf, sinf, limit, cache):
    return pl.pallas_call(
        attention_kernel,
        out_shape=jax.ShapeDtypeStruct((8, 256, 256), BF),
        in_specs=[VMEM] * 6 + [ANY],
        out_specs=VMEM,
        scratch_shapes=[
            pltpu.VMEM((2, 4096, 2, 128), BF),
            pltpu.VMEM((4096, 256), BF),
            pltpu.VMEM((2, 9, 256, 512), F32),
            pltpu.VMEM((2, 256, 128), F32),
            pltpu.VMEM((2, 256, 128), F32),
            pltpu.VMEM((2, 256, 128), F32),
            pltpu.VMEM((256, 2048), BF),
            DMA((8, 2)),
        ],
        compiler_params=pltpu.CompilerParams(vmem_limit_bytes=48 << 20),
        name="attention",
    )(tok, w, gain, cosf, sinf, limit, cache)


def scatter_sum_kernel(part, got, lsem, ssem, rsem):
    s, t = places()
    greet(tp_peers(s, t))
    local = pltpu.make_async_copy(part.at[t], got.at[t], lsem)
    local.start()
    copies = [push(part.at[t ^ k], got.at[t], ssem.at[k], rsem.at[k], (s, t ^ k)) for k in range(1, 8)]
    for copy in copies:
        copy.wait()
    local.wait()


def scatter_sum(part):
    return pl.pallas_call(
        scatter_sum_kernel,
        out_shape=jax.ShapeDtypeStruct((8, 256, 256), BF),
        in_specs=[ANY],
        out_specs=ANY,
        scratch_shapes=[DMA, DMA((8,)), DMA((8,))],
        compiler_params=pltpu.CompilerParams(collective_id=1, has_side_effects=True),
        name="project_exchange",
    )(part)


def slot_rows(rank, first):
    shelf = lax.broadcasted_iota(jnp.int32, (32, 256), 0).astype(F32)
    return [jnp.where(rank[first + e : first + e + 1, :] == shelf, 1.0, 0.0) for e in range(8)]


def send_rows_kernel(got, tok, rank, routes, router, gain, hidden, rows, stats):
    total = tok[...].astype(F32)
    part = got[0].astype(F32)
    for k in range(1, 8):
        part += got[k].astype(F32)
    state = (total + part).astype(BF)
    hidden[...] = state
    for chunk in range(8):
        pick = jnp.concatenate(slot_rows(rank, chunk * 8), axis=0).astype(BF)
        rows[chunk] = jnp.dot(pick, state, preferred_element_type=F32).astype(BF)
    wide = state.astype(F32)
    logits = nt(router[...], (wide * gain[...]).astype(BF))
    expert = lax.broadcasted_iota(jnp.int32, (64, 256), 0)
    lines = [
        jnp.sum(jnp.where(routes[k : k + 1, :] == expert, logits, 0.0), axis=0, keepdims=True)
        for k in range(6)
    ]
    square = jnp.sum(jnp.transpose(wide * wide), axis=0, keepdims=True)
    stats[...] = jnp.concatenate(lines + [square, jnp.zeros((1, 256), F32)], axis=0)


def send_rows(got, tok, rank, routes, router, gain):
    return pl.pallas_call(
        send_rows_kernel,
        out_shape=(
            jax.ShapeDtypeStruct((256, 256), BF),
            jax.ShapeDtypeStruct((8, 256, 256), BF),
            jax.ShapeDtypeStruct((8, 256), F32),
        ),
        in_specs=[VMEM] * 6,
        out_specs=(VMEM,) * 3,
        name="send_rows",
    )(got, tok, rank, routes, router, gain)


def dispatch_kernel(rows, stats, x, stats_all, stage, lsem, a_s, a_r, b_s, b_r, g_s, g_r):
    s, t = places()
    z, r = s // 4, s % 4
    far = [seq_peer(s, t, k, j) for k in range(8) for j in range(4) if (k, j) != (0, 0)]
    greet(tp_peers(s, t) + far)
    sends = []
    own = pltpu.make_async_copy(rows.at[:, s], stage.at[:, s], lsem.at[0])
    own.start()
    for k in ORDER:
        for j in range(4):
            if (k, j) == (0, 0):
                continue
            peer = seq_peer(s, t, k, j)
            sends.append(push(rows.at[:, peer[0]], stage.at[:, s], a_s.at[k, j], a_r.at[k, j], peer))
    small = [push(stats, stats_all.at[t], g_s.at[k], g_r.at[k], (s, t ^ k)) for k in range(1, 8)]
    near = pltpu.make_async_copy(stats, stats_all.at[t], lsem.at[1])
    near.start()
    columns = pl.ds(pl.multiple_of(t * 256, 256), 256)
    forwards = []
    locals_ = []
    for k in ORDER:
        group = (z + 8 - k) % 8
        here = pl.ds(group * 4, 4)
        for j in range(4):
            if (k, j) == (0, 0):
                own.wait()
            else:
                source = group * 4 + (r ^ j)
                pltpu.make_async_copy(stage.at[:, source], stage.at[:, source], a_r.at[k, j]).wait()
        target = x.at[here, :, columns]
        for m in range(1, 8):
            forwards.append(
                push(stage.at[(t ^ m) % 2, here], target, b_s.at[k, m], b_r.at[k, m], (s, t ^ m))
            )
        keep = pltpu.make_async_copy(stage.at[t % 2, here], target, b_s.at[k, 0])
        keep.start()
        locals_.append(keep)
    for copy in sends:
        copy.wait_send()
    for copy in forwards + small:
        copy.wait()
    for copy in locals_:
        copy.wait()
    near.wait()


def dispatch(rows, stats):
    return pl.pallas_call(
        dispatch_kernel,
        out_shape=(
            jax.ShapeDtypeStruct((32, 32, 2048), BF),
            jax.ShapeDtypeStruct((8, 8, 256), F32),
        ),
        in_specs=[ANY, ANY],
        out_specs=(ANY, ANY),
        scratch_shapes=[
            pltpu.VMEM((2, 32, 32, 256), BF),
            DMA((2,)),
            DMA((8, 4)),
            DMA((8, 4)),
            DMA((8, 8)),
            DMA((8, 8)),
            DMA((8,)),
            DMA((8,)),
        ],
        compiler_params=pltpu.CompilerParams(collective_id=2, has_side_effects=True),
        name="dispatch",
    )(rows, stats)


def experts_kernel(
    flags, x, gain, s_gu, s_down, a_gu, a_down, b_gu, b_down, y, wbuf, wdown, weights, xn, sem
):
    def fetch(gu, down, first, count, slot):
        copies = []
        for col in range(16):
            copies.append(
                pltpu.make_async_copy(
                    gu.at[:, :, pl.ds(col * 128, 128)],
                    wbuf.at[col, pl.ds(first, count)],
                    sem.at[slot, col],
                )
            )
        copies.append(
            pltpu.make_async_copy(down, wdown.at[pl.ds(first, count)], sem.at[slot, 16])
        )
        return copies

    fresh = flags[0] == 1
    low = pl.multiple_of(flags[1] * 176, 16)
    high = pl.multiple_of(176 - flags[1] * 176, 16)

    def both():
        return fetch(a_gu, a_down, low, 176, 0) + fetch(b_gu, b_down, high, 176, 1)

    def single():
        return fetch(s_gu, s_down, 0, 352, 0)

    @pl.when(fresh)
    def _():
        for copy in both():
            copy.start()

    @pl.when(jnp.logical_not(fresh))
    def _():
        for copy in single():
            copy.start()

    @pl.loop(0, 16)
    def _(i):
        span = pl.ds(pl.multiple_of(i * 64, 64), 64)
        field = x[span, :].astype(F32)
        inv = lax.rsqrt(jnp.mean(field * field, axis=-1, keepdims=True) + 1e-6)
        xn[span, :] = (field * inv * gain[...]).astype(BF)

    @pl.when(fresh)
    def _():
        for copy in both():
            copy.wait()

    @pl.when(jnp.logical_not(fresh))
    def _():
        for copy in single():
            copy.wait()

    flat = wbuf.reshape(16, 704, 128)
    for first, count in ((0, 256), (256, 256), (512, 192)):
        perm = split_matrix(count)
        half = count // 2
        for col in range(8):
            pair = jnp.concatenate(
                [flat[2 * col + i, first : first + count, :] for i in range(2)], axis=1
            )
            split = jnp.dot(perm, pair, preferred_element_type=F32).astype(BF)
            for kind in range(2):
                weights[kind, first // 2 : first // 2 + half, col * 256 : col * 256 + 256] = split[
                    kind * half : kind * half + half
                ]

    @pl.loop(0, 8)
    def _(i):
        span = pl.ds(pl.multiple_of(i * 128, 128), 128)
        block = xn[span, :]
        gate = nt(block, weights[0])
        up = nt(block, weights[1])
        act = (gate / (1.0 + jnp.exp(-gate)) * up).astype(BF)
        result = jnp.dot(act, wdown[...], preferred_element_type=F32).astype(BF)
        for part in range(8):
            y[part, span, :] = result[:, part * 256 : part * 256 + 256]


def experts(flags, x, gain, *weights):
    return pl.pallas_call(
        experts_kernel,
        out_shape=jax.ShapeDtypeStruct((8, 1024, 256), BF),
        in_specs=[SMEM, VMEM, VMEM] + [ANY] * 6,
        out_specs=VMEM,
        scratch_shapes=[
            pltpu.VMEM((16, 352, 2, 128), BF),
            pltpu.VMEM((352, 2048), BF),
            pltpu.VMEM((2, 352, 2048), BF),
            pltpu.VMEM((1024, 2048), BF),
            DMA((2, 17)),
        ],
        compiler_params=pltpu.CompilerParams(vmem_limit_bytes=48 << 20),
        name="experts",
    )(flags, x, gain, *weights)


def return_kernel(y, back, tbuf, sums, lsem, a_s, a_r, b_s, b_r):
    s, t = places()
    z, r = s // 4, s % 4
    far = [seq_peer(s, t, k, j) for k in range(8) for j in range(4) if (k, j) != (0, 0)]
    greet(tp_peers(s, t) + far)
    firsts, locals_ = [], []
    for k in ORDER:
        here = pl.ds(((z + k) % 8) * 4, 4)
        for m in range(1, 8):
            firsts.append(
                push(y.at[t ^ m, here], tbuf.at[t, here], a_s.at[k, m], a_r.at[k, m], (s, t ^ m))
            )
        keep = pltpu.make_async_copy(y.at[t, here], tbuf.at[t, here], lsem.at[k])
        keep.start()
        locals_.append(keep)
    seconds = []
    last = None
    for place, k in enumerate(ORDER):
        group = ((z + k) % 8) * 4
        here = pl.ds(group, 4)
        for copy in firsts[place * 7 : place * 7 + 7]:
            copy.wait_recv()
        locals_[place].wait()
        for par in range(2):
            first = tbuf[par, here].astype(F32) + tbuf[par + 2, here].astype(F32)
            second = tbuf[par + 4, here].astype(F32) + tbuf[par + 6, here].astype(F32)
            sums[par, here] = (first + second).astype(BF)
        for j in range(4):
            target = group + (r ^ j)
            if (k, j) == (0, 0):
                last = pltpu.make_async_copy(sums.at[:, target], back.at[:, s], lsem.at[8])
                last.start()
            else:
                seconds.append(
                    push(sums.at[:, target], back.at[:, s], b_s.at[k, j], b_r.at[k, j], (target, t))
                )
    for copy in firsts:
        copy.wait_send()
    for copy in seconds:
        copy.wait()
    last.wait()


def give_back(y):
    return pl.pallas_call(
        return_kernel,
        out_shape=jax.ShapeDtypeStruct((2, 32, 32, 256), BF),
        in_specs=[ANY],
        out_specs=ANY,
        scratch_shapes=[
            pltpu.VMEM((8, 32, 32, 256), BF),
            pltpu.VMEM((2, 32, 32, 256), BF),
            DMA((9,)),
            DMA((8, 8)),
            DMA((8, 8)),
            DMA((8, 4)),
            DMA((8, 4)),
        ],
        compiler_params=pltpu.CompilerParams(
            collective_id=3, has_side_effects=True, vmem_limit_bytes=24 << 20
        ),
        name="give_back",
    )(y)


def combine_kernel(back, hidden, rank, routes, stats, out):
    lines = stats[0]
    for k in range(1, 8):
        lines += stats[k]
    inv = lax.rsqrt(lines[6:7, :] * (1.0 / 2048.0) + 1e-6)
    gate = 1.0 / (1.0 + jnp.exp(-(lines * inv)))
    shelf = lax.broadcasted_iota(jnp.int32, (64, 256), 0)
    expert = (shelf % 32) * 2 + shelf // 32
    share = jnp.zeros((64, 256), F32)
    for k in range(6):
        share += jnp.where(routes[k : k + 1, :] == expert, gate[k : k + 1, :], 0.0)
    total = hidden[...].astype(F32)
    for chunk in range(8):
        pick = slot_rows(rank, chunk * 8)
        mix = jnp.concatenate(
            [pick[e] * share[chunk * 8 + e : chunk * 8 + e + 1, :] for e in range(8)], axis=0
        )
        high = mix.astype(BF)
        low = (mix - high.astype(F32)).astype(BF)
        dims = (((0,), (0,)), ((), ()))
        total += lax.dot_general(high, back[chunk], dims, preferred_element_type=F32)
        total += lax.dot_general(low, back[chunk], dims, preferred_element_type=F32)
    out[...] = total.astype(BF)


def combine(back, hidden, rank, routes, stats):
    return pl.pallas_call(
        combine_kernel,
        out_shape=jax.ShapeDtypeStruct((256, 256), BF),
        in_specs=[VMEM] * 5,
        out_specs=VMEM,
        name="combine",
    )(back, hidden, rank, routes, stats)


def swapped(array):
    return lax.ppermute(array, "tp", [(i, i ^ 1) for i in range(8)])


def body(
    tokens,
    ctx_len,
    cache_kv,
    cache_pos,
    attn_gain,
    moe_gain,
    qkv_train,
    out_train,
    router,
    routes,
    handed_half,
    fresh_gu,
    fresh_down,
    server_gu,
    server_down,
):
    t = lax.axis_index("tp")
    s = lax.axis_index("seq")
    own_gu = fresh_gu[0].astype(BF)
    own_down = fresh_down[0].astype(BF)
    other_gu, other_down = swapped((own_gu, own_down))
    shard = jnp.concatenate([qkv_train.reshape(64, 768), out_train], axis=1).astype(BF)
    tok_all, w_all = gather(tokens, shard)

    context = ctx_len[0]
    half = HEAD_DIM // 2
    frequency = 10000.0 ** (-jnp.arange(half, dtype=F32) / half)
    positions = context + jnp.arange(256, dtype=jnp.int32)
    angles = positions.astype(F32)[:, None] * frequency[None, :]
    cosine, sine = jnp.cos(angles), jnp.sin(angles)
    cosf = jnp.concatenate([cosine, cosine], axis=1)
    sinf = jnp.concatenate([-sine, sine], axis=1)
    slot = cache_pos
    limit = jnp.where(slot < 0, 0, jnp.where(slot < SINK, 256, slot + WIN - context))
    part = attention(
        tok_all,
        w_all.reshape(2048, 1024),
        attn_gain.reshape(1, 2048),
        cosf,
        sinf,
        limit,
        cache_kv[0],
    )
    got = scatter_sum(part)

    routes_t = routes.T
    shelf = jnp.arange(64, dtype=jnp.int32)
    named = (shelf % 32) * 2 + shelf // 32
    hit = jnp.any(routes_t[None, :, :] == named[:, None, None], axis=1)
    later = (jnp.arange(256)[:, None] < jnp.arange(256)[None, :]).astype(BF)
    before = jnp.dot(hit.astype(BF), later, preferred_element_type=F32)
    rank = jnp.where(hit, before, -1.0)

    columns = t * 256
    gain_part = lax.dynamic_slice_in_dim(moe_gain, columns, 256, 0).reshape(1, 256)
    router_part = lax.dynamic_slice_in_dim(router, columns, 256, 0).T
    hidden, rows, stats = send_rows(got, tokens, rank, routes_t, router_part, gain_part)
    x, stats_all = dispatch(rows.reshape(2, 32, 32, 256), stats)

    parity = t % 2
    use_fresh = lax.dynamic_index_in_dim(handed_half, s, 0, keepdims=False) == parity
    flags = jnp.stack([use_fresh.astype(jnp.int32), parity.astype(jnp.int32)])
    y = experts(
        flags,
        x.reshape(1024, 2048),
        moe_gain.reshape(1, 2048),
        server_gu[0],
        server_down[0],
        own_gu,
        own_down,
        other_gu,
        other_down,
    )
    back = give_back(y.reshape(8, 32, 32, 256))
    return combine(back.reshape(8, 256, 256), hidden, rank, routes_t, stats_all)


def solution(mesh):
    placed = (
        P("seq", "tp"),
        P("seq"),
        P("seq", None, None, "tp"),
        P("seq", None),
        P(),
        P(),
        P("seq", None, "tp"),
        P("seq", "tp"),
        P(),
        P("seq", None),
        P(),
        P("seq", "tp", None, None),
        P("seq", "tp", None),
        P("seq", "tp", None, None),
        P("seq", "tp", None),
    )
    return jax.shard_map(
        body, mesh=mesh, in_specs=placed, out_specs=P("seq", "tp"), check_vma=False
    )
```

time: 696 us -> 279 us (0.40)
  waiting for transfers between devices: 488 us -> 0.01 us
  Pallas kernels: 0 us -> 259 us
  local copies, waits for them, and re-layouts: 76.1 us -> 8.63 us
  other arithmetic: 60.2 us -> 6.28 us
  matrix products: 29.1 us -> 0.79 us
  starting transfers between devices: 27 us -> 2.32 us
  between operations: 14.8 us -> 1.46 us
    pallas_call x0 -> x8, Pallas kernels: none -> 259 us  [the longest x1 74.4 us: give_back(): pl.pallas_call(return_kernel, out_shape=jax.ShapeDtypeStruct((2, 32, 32,...]
    all_gather x3 -> x0, waiting for transfers between devices: 165 us -> none  [the longest x1 90.5 us: body(): lax.all_gather(qkv_train.astype(jnp.bfloat16), 'seq', axis=0, tiled=True)]
    all_to_all x2 -> x0, waiting for transfers between devices: 148 us -> none  [the longest x1 134 us: body(): lax.all_to_all(outgoing, 'seq', split_axis=0, concat_axis=0, tiled=True)]
    reduce_scatter x1 -> x0, waiting for transfers between devices: 90.4 us -> none  [body(): lax.psum_scatter(placed.astype(jnp.bfloat16), 'tp', scatter_dimension=3,...]
    psum x1 -> x0, waiting for transfers between devices: 53.8 us -> none  [body(): lax.psum(partial_out.astype(jnp.bfloat16), 'tp').astype(jnp.float32)]
    another operation x5 -> x2, other arithmetic: 34.6 us -> 0.08 us  [the longest x1 0.08 us: body(): flags = jnp.stack([use_fresh.astype(jnp.int32), parity.astype(jnp.int32)])]
    ppermute x2, waiting for transfers between devices: 30.2 us -> 0.01 us  [swapped(): return lax.ppermute(array, 'tp', [(i, i ^ 1) for i in range(8)])]
    dot_general x7 -> x1, matrix products: 29.1 us -> 0.79 us  [body(): before = jnp.dot(hit.astype(BF), later, preferred_element_type=F32)]
  transfers between devices with their start and end apart: 9 -> 2, of which waited for: 8 -> 0; matrix products, arithmetic and copies ran while one was open for 15% -> 3% of each run, Pallas kernels for 0% -> 57%
where the time goes in v1:
time: 279 us
  Pallas kernels  259 us (93%)
  local copies, waits for them, and re-layouts  8.63 us (3%)
  other arithmetic  6.28 us (2%)
    pallas_call x1, Pallas kernels, give_back(): pl.pallas_call(return_kernel, out_shape=jax.ShapeDtypeStruct((2, 32, 32,...  74.4 us
    pallas_call x1, Pallas kernels, dispatch(): pl.pallas_call(dispatch_kernel, out_shape=(jax.ShapeDtypeStruct((32, 32,...  74.3 us
    pallas_call x1, Pallas kernels, gather(): pl.pallas_call(gather_kernel, out_shape=(jax.ShapeDtypeStruct((256, 2048)...  54.6 us
    pallas_call x1, Pallas kernels, experts(): pl.pallas_call(experts_kernel, out_shape=jax.ShapeDtypeStruct((8, 1024, 2...  22.2 us
    pallas_call x1, Pallas kernels, scatter_sum(): pl.pallas_call(scatter_sum_kernel, out_shape=jax.ShapeDtypeStruct((8, 256...  14.5 us
    pallas_call x1, Pallas kernels, attention(): pl.pallas_call(attention_kernel, out_shape=jax.ShapeDtypeStruct((8, 256,...  13.5 us
    unnamed x26, local copies, waits for them, and re-layouts  6.77 us
  transfers between devices with their start and end apart: 2, of which 0 were waited for; matrix products, arithmetic and copies ran while one was open for 3% of the time, Pallas kernels for 57%

profile of v1, /device:TPU:1, one launch (start us, length us, event | category | flops | bytes accessed | tf_op | source)
XLA Modules:
  0.0 278.6 jit_solution(15194436963097525532)
XLA Ops:
  0.0 1.5 convert_bitcast_fusion.1.a_down
  1.5 0.0 copy-start.11
  1.5 0.0 copy-start.12
  1.6 0.0 copy-start.7
  1.6 2.2 collective-permute-start.1
  3.8 3.2 %convert_bitcast_fusion.a_gu = bf16[176,2,2048]{2,1,0:T(2,128)(2,1)S(1)} fusion(f32[1,176,2,2048]{3,2,1,0:T(2,128)} %param.26), kind=kLoop, calls=%fused_computation | loop fusion | flops 720896 | bytes 4325376 | tf_op jit(solution)/shard_map/convert_element_type | solution.py:602
  7.0 0.1 collective-permute-start
  7.8 0.0 copy-done.8
  7.8 0.5 fusion
  8.4 0.1 pad_maximum_fusion.1
  8.5 0.7 pad_maximum_fusion.w
  9.2 0.6 dynamic_slice.10
  10.4 54.6 %gather_inputs.1 = (bf16[256,2048]{1,0:T(8,128)(2,1)}, bf16[8,2,2,64,1024]{4,3,2,1,0:T(8,128)(2,1)}) custom-call(bf16[256,256]{1,0:T(8,128)(2,1)} %tok.3, bf16[64,1024]{1,0:T(8,128)(2,1)} %pad_maximum_fusion.w), custom_call_target="tpu_custom_call" | custom-call | tf_op jit(solution)/shard_map/gather_inputs/pallas_call | solution.py:104
  65.0 1.2 copy-done.5
  66.2 13.5 %attention.1.part = bf16[8,256,256]{2,1,0:T(8,128)(2,1)S(1)} custom-call(bf16[256,2048]{1,0:T(8,128)(2,1)S(1)} %copy-done.5, bf16[2048,1024]{1,0:T(8,128)(2,1)} %bitcast.35, f32[1,2048]{1,0:T(1,128)S(1)} %bitcast.32, f32[256,128]{1,0:T(8,128)S(1)} %get-tuple-element.22.cosf, f32[256,128]{1,0:T(8,128)S(1)} %get-tuple-element.23.sinf, ...), custom_call_target="tpu_custom_call" | custom-call | tf_op jit(solution)/shard_map/attention/pallas_call | solution.py:227
  79.7 1.0 copy-done.3
  80.7 14.5 %project_exchange.1.got = bf16[8,256,256]{2,1,0:T(8,128)(2,1)} custom-call(bf16[8,256,256]{2,1,0:T(8,128)(2,1)} %copy-done.3), custom_call_target="tpu_custom_call" | custom-call | tf_op jit(solution)/shard_map/project_exchange/pallas_call | solution.py:259
  95.2 0.6 dynamic_slice.12
  95.9 0.6 dynamic-slice_bitcast_fusion.router
  96.5 0.1 compare_reduce_fusion
  96.6 0.8 convolution_select_fusion.rank
  97.4 2.9 %send_rows.1 = (bf16[256,256]{1,0:T(8,128)(2,1)}, bf16[8,256,256]{2,1,0:T(8,128)(2,1)}, f32[8,256]{1,0:T(8,128)}) custom-call(bf16[8,256,256]{2,1,0:T(8,128)(2,1)} %project_exchange.1.got, bf16[256,256]{1,0:T(8,128)(2,1)} %tok.3, f32[64,256]{1,0:T(8,128)} %convolution_select_fusion.rank, s32[6,256]{1,0:T(8,128)} %bitcast.39, ...), custom_call_target="tpu_custom_call" | custom-call | tf_op jit(solution)/shard_map/send_rows/pallas_call | solution.py:297
  100.3 74.3 %dispatch.1 = (bf16[32,32,2048]{2,1,0:T(8,128)(2,1)}, f32[8,8,256]{2,1,0:T(8,128)}) custom-call(bf16[2,32,32,256]{3,2,1,0:T(8,128)(2,1)} %bitcast.37, f32[8,256]{1,0:T(8,128)} %get-tuple-element.15.stats), custom_call_target="tpu_custom_call" | custom-call | tf_op jit(solution)/shard_map/dispatch/pallas_call | solution.py:357
  174.6 0.1 pad_add_fusion.flags
  174.7 0.0 collective-permute-done.1.b_down
  174.7 0.0 collective-permute-done.b_gu
  174.7 1.4 copy-done.4
  176.0 22.2 %experts.1 = bf16[8,1024,256]{2,1,0:T(8,128)(2,1)} custom-call(s32[2]{0:T(128)S(1)} %pad_add_fusion.flags, bf16[1024,2048]{1,0:T(8,128)(2,1)} %bitcast.33, f32[1,2048]{1,0:T(1,128)S(1)} %bitcast.31, bf16[352,2,2048]{2,1,0:T(2,128)(2,1)} %bitcast.36, bf16[352,2048]{1,0:T(8,128)(2,1)S(1)} %bitcast.30, bf16[176,2,2048]{2,1,0:T(2,128)(2,1)S(1)} %convert_bitcast_fusion.a_gu, ...), custom_call_target="tpu_custom_call" | custom-call | tf_op jit(solution)/shard_map/experts/pallas_call | solution.py:462
  198.2 2.2 copy-done.1
  200.4 74.4 %give_back.1 = bf16[2,32,32,256]{3,2,1,0:T(8,128)(2,1)S(1)} custom-call(bf16[8,32,32,256]{3,2,1,0:T(8,128)(2,1)S(1)} %bitcast.28), custom_call_target="tpu_custom_call" | custom-call | tf_op jit(solution)/shard_map/give_back/pallas_call | solution.py:523
  274.8 1.0 copy-done.2
  275.8 2.8 combine.1
  (24 shorter events, 0.1 us)
Async XLA Ops:
  0.0 95.9 %copy-start = (bf16[2048,64]{0,1:T(8,128)(2,1)S(1)}, bf16[2048,64]{0,1:T(8,128)(2,1)}, u32[]{:S(2)}) copy-start(bf16[2048,64]{0,1:T(8,128)(2,1)} %param.23) | copy-start | bytes 786436
  0.0 7.7 %copy-start.10 = (f32[64,256]{1,0:T(8,128)S(1)}, f32[64,256]{1,0:T(8,128)}, u32[]{:S(2)}) copy-start(f32[64,256]{1,0:T(8,128)} %param.22) | copy-start | bytes 196612
  0.0 7.8 %copy-start.8 = (f32[64,3,256]{2,0,1:T(8,128)S(1)}, f32[64,3,256]{2,0,1:T(8,128)}, u32[]{:S(2)}) copy-start(f32[64,3,256]{2,0,1:T(8,128)} %param.21) | copy-start | bytes 589828
  1.5 7.0 %copy-start.11 = (s32[1,4096]{1,0:T(1,128)S(1)}, s32[1,4096]{1,0:T(1,128)}, u32[]{:S(2)}) copy-start(s32[1,4096]{1,0:T(1,128)} %param.18) | copy-start | bytes 49156
  1.5 7.7 %copy-start.12 = (s32[32]{0:T(128)S(1)}, s32[32]{0:T(128)}, u32[]{:S(2)}) copy-start(s32[32]{0:T(128)} %param.25) | copy-start | bytes 388
  1.6 63.4 %copy-start.7 = (f32[2048]{0:T(1024)S(1)}, f32[2048]{0:T(1024)}, u32[]{:S(2)}) copy-start(f32[2048]{0:T(1024)} %param.19) | copy-start | bytes 24580
  1.6 173.1 %collective-permute-start.1 = (bf16[176,2048]{1,0:T(8,128)(2,1)S(1)}, bf16[176,2048]{1,0:T(8,128)(2,1)S(1)}, u32[]{:S(2)}, u32[]{:S(2)}) collective-permute-start(bf16[176,2048]{1,0:T(8,128)(2,1)S(1)} %convert_bitcast_fusion.1.a_down), channel_id=1, source_target_pairs={{0,1},{1,0},{2,3},{3,2},{4,5},{5,4},{6,7},{7,6},{8,9},{9,8},{10,11... | collective-permute-start | bytes 2162696 | tf_op jit(solution)/shard_map/ppermute | solution.py:580
  7.0 167.7 %collective-permute-start = (bf16[176,2,2048]{2,1,0:T(2,128)(2,1)S(1)}, bf16[176,2,2048]{2,1,0:T(2,128)(2,1)}, u32[]{:S(2)}, u32[]{:S(2)}) collective-permute-start(bf16[176,2,2048]{2,1,0:T(2,128)(2,1)S(1)} %convert_bitcast_fusion.a_gu), channel_id=1, source_target_pairs={{0,1},{1,0},{2,3},{3,2},{4,5},{5,4},{6,7},{7,6},{8,9},{9,8},{10,11... | collective-permute-start | bytes 4325384 | tf_op jit(solution)/shard_map/ppermute | solution.py:580
  65.0 1.2 copy-start.5
  66.2 29.0 %copy-start.6 = (f32[2048]{0:T(1024)S(1)}, f32[2048]{0:T(1024)}, u32[]{:S(2)}) copy-start(f32[2048]{0:T(1024)} %param.20) | copy-start | bytes 24580
  66.2 30.3 %copy-start.9 = (s32[256,6]{0,1:T(8,128)S(1)}, s32[256,6]{0,1:T(8,128)}, u32[]{:S(2)}) copy-start(s32[256,6]{0,1:T(8,128)} %param.24) | copy-start | bytes 18436
  79.7 1.0 copy-start.3
  174.7 1.4 copy-start.4
  198.2 2.2 copy-start.1
  274.8 1.0 copy-start.2

commit v2 on v1

--- a/solution.py
+++ b/solution.py
@@ -17,7 +17,6 @@
 VMEM = pl.BlockSpec(memory_space=pltpu.VMEM)
 SMEM = pl.BlockSpec(memory_space=pltpu.SMEM)
 DMA = pltpu.SemaphoreType.DMA
-ORDER = (0, 1, 7, 2, 6, 3, 5, 4)
 
 
 def places():
@@ -31,10 +30,14 @@
     pl.semaphore_wait(barrier, len(peers))
 
 
-def push(src, dst, send, recv, peer):
-    copy = pltpu.make_async_remote_copy(
+def remote(src, dst, send, recv, peer):
+    return pltpu.make_async_remote_copy(
         src_ref=src, dst_ref=dst, send_sem=send, recv_sem=recv, device_id=peer, device_id_type=MESH
     )
+
+
+def push(src, dst, send, recv, peer):
+    copy = remote(src, dst, send, recv, peer)
     copy.start()
     return copy
 
@@ -48,13 +51,56 @@
     return ((z + k) % 8) * 4 + (r ^ j), t
 
 
-def gather_kernel(tok, w, tok_all, w_all, lsem, tok_s, tok_r, x_s, x_r, z_s, z_r, c_s, c_r):
+def split_matrix(n):
+    row = lax.broadcasted_iota(jnp.int32, (n, n), 0)
+    col = lax.broadcasted_iota(jnp.int32, (n, n), 1)
+    half = n // 2
+    return jnp.where(col == jnp.where(row < half, 2 * row, 2 * (row - half) + 1), 1.0, 0.0).astype(BF)
+
+
+def gather_kernel(
+    tok,
+    qkv,
+    proj,
+    f_gu,
+    f_down,
+    s_gu,
+    tok_all,
+    w_all,
+    f_gu_out,
+    f_down_out,
+    s_gu_out,
+    w,
+    fbuf,
+    sbuf,
+    lsem,
+    tok_s,
+    tok_r,
+    x_s,
+    x_r,
+    z_s,
+    z_r,
+    c_s,
+    c_r,
+    p_s,
+):
     s, t = places()
     z, xh, c = s // 4, (s // 2) % 2, s % 2
     up = (((z + 1) % 8) * 4 + xh * 2 + c, t)
     down = (((z + 7) % 8) * 4 + xh * 2 + c, t)
     over = (s ^ 2, t)
     twin = (s ^ 1, t)
+
+    pulls = []
+    for col in range(16):
+        span = pl.ds(col * 128, 128)
+        pulls.append(pltpu.make_async_copy(f_gu.at[:, :, span], fbuf.at[col], p_s.at[0, col]))
+    for col in range(16):
+        span = pl.ds(col * 128, 128)
+        pulls.append(pltpu.make_async_copy(s_gu.at[:, :, span], sbuf.at[col], p_s.at[1, col]))
+    for j in range(3):
+        w[:, j * 256 : j * 256 + 256] = qkv[j].astype(BF)
+    w[:, 768:1024] = proj[...].astype(BF)
     greet(tp_peers(s, t) + [up, down, over, twin])
 
     def block(dz, a):
@@ -72,6 +118,39 @@
     local_t = pltpu.make_async_copy(tok, mine, lsem.at[1])
     local_t.start()
     toks = [push(tok, mine, tok_s.at[k], tok_r.at[k], (s, t ^ k)) for k in range(1, 8)]
+    for pull in pulls:
+        pull.start()
+
+    f_flat = fbuf.reshape(16, 352, 128)
+    s_flat = sbuf.reshape(16, 704, 128)
+
+    def part_fresh(first):
+        for col in range(first, first + 4):
+            pulls[col].wait()
+            for kind in range(2):
+                f_gu_out[kind, :, col * 128 : col * 128 + 128] = f_flat[
+                    col, pl.ds(kind, 176, stride=2), :
+                ].astype(BF)
+
+    def part_down():
+        f_down_out[...] = f_down[...].astype(BF)
+
+    def part_server(col):
+        for pull in pulls[16 + 2 * col : 18 + 2 * col]:
+            pull.wait()
+        for first, count in ((0, 256), (256, 256), (512, 192)):
+            half = count // 2
+            pair = jnp.concatenate(
+                [s_flat[2 * col + i, first : first + count, :] for i in range(2)], axis=1
+            )
+            split = jnp.dot(split_matrix(count), pair, preferred_element_type=F32).astype(BF)
+            for kind in range(2):
+                s_gu_out[kind, first // 2 : first // 2 + half, col * 256 : col * 256 + 256] = split[
+                    kind * half : kind * half + half
+                ]
+
+    work = [functools.partial(part_fresh, 4 * i) for i in range(4)] + [part_down]
+    work += [functools.partial(part_server, col) for col in range(8)]
 
     waits[0].wait_recv()
     theirs = block(0, 1)
@@ -84,6 +163,8 @@
             for way, (chain, peer, dz) in enumerate(((ups, up, -1 - step), (downs, down, 1 + step))):
                 if (step, a) not in chain:
                     continue
+                if work:
+                    work.pop(0)()
                 chain[(step, a)].wait_recv()
                 here = block(dz + 8, a)
                 if step < 2 or (step == 2 and a == way):
@@ -92,6 +173,8 @@
                     )
                 place = (dz + 8) % 8
                 twins.append(push(here, here, c_s.at[place, a], c_r.at[place, a], twin))
+    for piece in work:
+        piece()
     for copy in twins + toks:
         copy.wait()
     for copy in list(ups.values()) + list(downs.values()) + waits:
@@ -100,16 +183,22 @@
     local_t.wait()
 
 
-def gather(tok, w):
+def gather(tok, qkv, proj, f_gu, f_down, s_gu):
     return pl.pallas_call(
         gather_kernel,
         out_shape=(
             jax.ShapeDtypeStruct((256, 2048), BF),
             jax.ShapeDtypeStruct((8, 2, 2, 64, 1024), BF),
+            jax.ShapeDtypeStruct((2, 176, 2048), BF),
+            jax.ShapeDtypeStruct((176, 2048), BF),
+            jax.ShapeDtypeStruct((2, 352, 2048), BF),
         ),
-        in_specs=[ANY, ANY],
-        out_specs=(ANY, ANY),
+        in_specs=[VMEM, VMEM, VMEM, ANY, VMEM, ANY],
+        out_specs=(VMEM,) * 5,
         scratch_shapes=[
+            pltpu.VMEM((64, 1024), BF),
+            pltpu.VMEM((16, 176, 2, 128), F32),
+            pltpu.VMEM((16, 352, 2, 128), BF),
             DMA((2,)),
             DMA((8,)),
             DMA((8,)),
@@ -119,17 +208,13 @@
             DMA((2, 4, 2)),
             DMA((8, 2)),
             DMA((8, 2)),
+            DMA((2, 16)),
         ],
-        compiler_params=pltpu.CompilerParams(collective_id=0, has_side_effects=True),
+        compiler_params=pltpu.CompilerParams(
+            collective_id=0, has_side_effects=True, vmem_limit_bytes=28 << 20
+        ),
         name="gather_inputs",
-    )(tok, w)
-
-
-def split_matrix(n):
-    row = lax.broadcasted_iota(jnp.int32, (n, n), 0)
-    col = lax.broadcasted_iota(jnp.int32, (n, n), 1)
-    half = n // 2
-    return jnp.where(col == jnp.where(row < half, 2 * row, 2 * (row - half) + 1), 1.0, 0.0).astype(BF)
+    )(tok, qkv, proj, f_gu, f_down, s_gu)
 
 
 def nt(a, b):
@@ -239,7 +324,7 @@
             pltpu.VMEM((256, 2048), BF),
             DMA((8, 2)),
         ],
-        compiler_params=pltpu.CompilerParams(vmem_limit_bytes=48 << 20),
+        compiler_params=pltpu.CompilerParams(vmem_limit_bytes=30 << 20),
         name="attention",
     )(tok, w, gain, cosf, sinf, limit, cache)
 
@@ -259,8 +344,8 @@
     return pl.pallas_call(
         scatter_sum_kernel,
         out_shape=jax.ShapeDtypeStruct((8, 256, 256), BF),
-        in_specs=[ANY],
-        out_specs=ANY,
+        in_specs=[VMEM],
+        out_specs=VMEM,
         scratch_shapes=[DMA, DMA((8,)), DMA((8,))],
         compiler_params=pltpu.CompilerParams(collective_id=1, has_side_effects=True),
         name="project_exchange",
@@ -307,238 +392,291 @@
     )(got, tok, rank, routes, router, gain)
 
 
-def dispatch_kernel(rows, stats, x, stats_all, stage, lsem, a_s, a_r, b_s, b_r, g_s, g_r):
+def moe_kernel(
+    rows,
+    stats,
+    flag,
+    gain,
+    s_gu,
+    s_down,
+    a_gu,
+    a_down,
+    b_gu,
+    b_down,
+    back,
+    stats_all,
+    stage,
+    xstage,
+    x,
+    y,
+    ybuf,
+    halves,
+    xbuf,
+    sums,
+    w_gu,
+    w_down,
+    lsem,
+    g_s,
+    g_r,
+    d_s,
+    d_r,
+    dx_s,
+    dx_r,
+    dy_s,
+    dy_r,
+    ry_s,
+    ry_r,
+    rx_s,
+    rx_r,
+    r_s,
+    r_r,
+):
     s, t = places()
     z, r = s // 4, s % 4
+    side, mine = t // 4, t % 2
+    cross = (s, t ^ 4)
     far = [seq_peer(s, t, k, j) for k in range(8) for j in range(4) if (k, j) != (0, 0)]
     greet(tp_peers(s, t) + far)
-    sends = []
-    own = pltpu.make_async_copy(rows.at[:, s], stage.at[:, s], lsem.at[0])
-    own.start()
-    for k in ORDER:
+
+    def distance(i):
+        return jnp.where(i % 2 == 1, (i + 1) // 2, (8 - i // 2) % 8)
+
+    def arriving(i, j):
+        source = ((z + 8 - distance(i)) % 8) * 4 + (r ^ j)
+        return remote(rows.at[:, source], stage.at[:, source], d_s.at[i, j], d_r.at[i, j], (s, t ^ 1))
+
+    def leaving(i, j):
+        target = ((z + distance(i)) % 8) * 4 + (r ^ j)
+        return remote(rows.at[:, target], stage.at[:, s], d_s.at[i, j], d_r.at[i, j], (target, t))
+
+    def group(i):
+        return pl.ds(((z + 8 - distance(i)) % 8) * 4, 4)
+
+    def crossing(i):
+        here = group(i)
+        return remote(stage.at[:, here], xstage.at[:, here], dx_s.at[i], dx_r.at[i], cross)
+
+    def columns(which):
+        owner = t ^ (4 * which)
+        return pl.ds(pl.multiple_of(owner * 256, 256), 256)
+
+    def spreading(i, which, m):
+        here = group(i)
+        buf = (stage, xstage)[which]
+        return remote(
+            buf.at[(t ^ m) % 2, here],
+            x.at[here, :, columns(which)],
+            dy_s.at[i, which, m],
+            dy_r.at[i, which, m],
+            (s, t ^ m),
+        )
+
+    def keeping(i, which):
+        here = group(i)
+        buf = (stage, xstage)[which]
+        return pltpu.make_async_copy(
+            buf.at[mine, here], x.at[here, :, columns(which)], dy_s.at[i, which, 0]
+        )
+
+    def sharing(i, m):
+        here = group(i)
+        return remote(
+            y.at[:, (t ^ m) % 4, here], ybuf.at[m - 1, :, here], ry_s.at[i, m], ry_r.at[i, m], (s, t ^ m)
+        )
+
+    def joining(i):
+        here = group(i)
+        return remote(halves.at[1 - side, :, here], xbuf.at[:, here], rx_s.at[i], rx_r.at[i], cross)
+
+    def returning(i, j):
+        target = ((z + 8 - distance(i)) % 8) * 4 + (r ^ j)
+        return remote(sums.at[:, target], back.at[:, s], r_s.at[i, j], r_r.at[i, j], (target, t))
+
+    own_in = pltpu.make_async_copy(rows.at[:, s], stage.at[:, s], lsem.at[0])
+    own_out = pltpu.make_async_copy(sums.at[:, s], back.at[:, s], lsem.at[1])
+    own_in.start()
+    for j in range(1, 4):
+        leaving(0, j).start()
+
+    @pl.loop(1, 8)
+    def _(i):
         for j in range(4):
-            if (k, j) == (0, 0):
-                continue
-            peer = seq_peer(s, t, k, j)
-            sends.append(push(rows.at[:, peer[0]], stage.at[:, s], a_s.at[k, j], a_r.at[k, j], peer))
-    small = [push(stats, stats_all.at[t], g_s.at[k], g_r.at[k], (s, t ^ k)) for k in range(1, 8)]
-    near = pltpu.make_async_copy(stats, stats_all.at[t], lsem.at[1])
+            leaving(i, j).start()
+
+    def statistics(k):
+        return remote(stats, stats_all.at[t], g_s.at[k], g_r.at[k], (s, t ^ k))
+
+    near = pltpu.make_async_copy(stats, stats_all.at[t], lsem.at[2])
     near.start()
-    columns = pl.ds(pl.multiple_of(t * 256, 256), 256)
-    forwards = []
-    locals_ = []
-    for k in ORDER:
-        group = (z + 8 - k) % 8
-        here = pl.ds(group * 4, 4)
+    for k in range(1, 8):
+        statistics(k).start()
+
+    chosen = flag[...] > 0.0
+
+    def choose(mask, new, old):
+        return jnp.where(mask, new, old)
+
+    for first, gu, down in ((mine * 176, a_gu, a_down), (176 - mine * 176, b_gu, b_down)):
+
+        @pl.loop(0, 11)
+        def _(i):
+            here = pl.ds(pl.multiple_of(i * 16, 16), 16)
+            there = pl.ds(pl.multiple_of(first + i * 16, 16), 16)
+            for kind in range(2):
+                w_gu[kind, there, :] = choose(
+                    chosen, gu[kind, here, :].astype(F32), s_gu[kind, there, :].astype(F32)
+                ).astype(BF)
+            w_down[there, :] = choose(
+                chosen, down[here, :].astype(F32), s_down[there, :].astype(F32)
+            ).astype(BF)
+
+    def arrive(i):
+        @pl.when(i == 0)
+        def _():
+            own_in.wait()
+
+        @pl.when(i > 0)
+        def _():
+            arriving(i, 0).wait_recv()
+
+        for j in range(1, 4):
+            arriving(i, j).wait_recv()
+        crossing(i).start()
+        for m in range(1, 4):
+            spreading(i, 0, m).start()
+        keeping(i, 0).start()
+
+    def spread(i):
+        crossing(i).wait_recv()
+        for m in range(1, 4):
+            spreading(i, 1, m).start()
+        keeping(i, 1).start()
+
+    def compute(i):
+        for which in range(2):
+            for m in range(1, 4):
+                spreading(i, which, m).wait_recv()
+            keeping(i, which).wait()
+        here = group(i)
+        field = x[here].reshape(128, 2048).astype(F32)
+        inv = lax.rsqrt(jnp.mean(field * field, axis=-1, keepdims=True) + 1e-6)
+        block = (field * inv * gain[...]).astype(BF)
+        gate = nt(block, w_gu[0])
+        lift = nt(block, w_gu[1])
+        act = (gate / (1.0 + jnp.exp(-gate)) * lift).astype(BF)
+        for part in range(8):
+            result = jnp.dot(
+                act, w_down[:, part * 256 : part * 256 + 256], preferred_element_type=F32
+            )
+            y[part // 4, part % 4, here] = result.astype(BF).reshape(4, 32, 256)
+        for m in range(1, 4):
+            sharing(i, m).start()
+
+    def fold(i):
+        here = group(i)
+        for m in range(1, 4):
+            sharing(i, m).wait_recv()
+        for col in range(2):
+            same = y[col, t % 4, here].astype(F32) + ybuf[1, col, here].astype(F32)
+            halves[col, mine, here] = same.astype(BF)
+            other = ybuf[0, col, here].astype(F32) + ybuf[2, col, here].astype(F32)
+            halves[col, 1 - mine, here] = other.astype(BF)
+        joining(i).start()
+
+    def finish(i):
+        here = group(i)
+        joining(i).wait_recv()
+        for par in range(2):
+            total = halves[side, par, here].astype(F32) + xbuf[par, here].astype(F32)
+            sums[par, here] = total.astype(BF)
+
+        @pl.when(i == 0)
+        def _():
+            own_out.start()
+
+        @pl.when(i > 0)
+        def _():
+            returning(i, 0).start()
+
+        for j in range(1, 4):
+            returning(i, j).start()
+
+    @pl.loop(0, 12)
+    def _(i):
+        for lag, stage_of in enumerate((arrive, spread, compute, fold, finish)):
+
+            @pl.when((i >= lag) & (i < lag + 8))
+            def _():
+                stage_of(i - lag)
+
+    own_out.wait()
+    near.wait()
+    for k in range(1, 8):
+        statistics(k).wait()
+
+    def settle(i, j):
+        leaving(i, j).wait_send()
+        returning(i, j).wait()
+
+    for j in range(1, 4):
+        settle(0, j)
+
+    @pl.loop(1, 8)
+    def _(i):
         for j in range(4):
-            if (k, j) == (0, 0):
-                own.wait()
-            else:
-                source = group * 4 + (r ^ j)
-                pltpu.make_async_copy(stage.at[:, source], stage.at[:, source], a_r.at[k, j]).wait()
-        target = x.at[here, :, columns]
-        for m in range(1, 8):
-            forwards.append(
-                push(stage.at[(t ^ m) % 2, here], target, b_s.at[k, m], b_r.at[k, m], (s, t ^ m))
-            )
-        keep = pltpu.make_async_copy(stage.at[t % 2, here], target, b_s.at[k, 0])
-        keep.start()
-        locals_.append(keep)
-    for copy in sends:
-        copy.wait_send()
-    for copy in forwards + small:
-        copy.wait()
-    for copy in locals_:
-        copy.wait()
-    near.wait()
-
-
-def dispatch(rows, stats):
+            settle(i, j)
+
+    @pl.loop(0, 8)
+    def _(i):
+        crossing(i).wait_send()
+        joining(i).wait_send()
+        for m in range(1, 4):
+            sharing(i, m).wait_send()
+            for which in range(2):
+                spreading(i, which, m).wait_send()
+
+
+def moe(*operands):
     return pl.pallas_call(
-        dispatch_kernel,
+        moe_kernel,
         out_shape=(
-            jax.ShapeDtypeStruct((32, 32, 2048), BF),
+            jax.ShapeDtypeStruct((2, 32, 32, 256), BF),
             jax.ShapeDtypeStruct((8, 8, 256), F32),
         ),
-        in_specs=[ANY, ANY],
-        out_specs=(ANY, ANY),
+        in_specs=[VMEM] * 10,
+        out_specs=(VMEM, VMEM),
         scratch_shapes=[
             pltpu.VMEM((2, 32, 32, 256), BF),
-            DMA((2,)),
+            pltpu.VMEM((2, 32, 32, 256), BF),
+            pltpu.VMEM((32, 32, 2048), BF),
+            pltpu.VMEM((2, 4, 32, 32, 256), BF),
+            pltpu.VMEM((3, 2, 32, 32, 256), BF),
+            pltpu.VMEM((2, 2, 32, 32, 256), BF),
+            pltpu.VMEM((2, 32, 32, 256), BF),
+            pltpu.VMEM((2, 32, 32, 256), BF),
+            pltpu.VMEM((2, 352, 2048), BF),
+            pltpu.VMEM((352, 2048), BF),
+            DMA((3,)),
+            DMA((8,)),
+            DMA((8,)),
             DMA((8, 4)),
             DMA((8, 4)),
-            DMA((8, 8)),
-            DMA((8, 8)),
             DMA((8,)),
             DMA((8,)),
-        ],
-        compiler_params=pltpu.CompilerParams(collective_id=2, has_side_effects=True),
-        name="dispatch",
-    )(rows, stats)
-
-
-def experts_kernel(
-    flags, x, gain, s_gu, s_down, a_gu, a_down, b_gu, b_down, y, wbuf, wdown, weights, xn, sem
-):
-    def fetch(gu, down, first, count, slot):
-        copies = []
-        for col in range(16):
-            copies.append(
-                pltpu.make_async_copy(
-                    gu.at[:, :, pl.ds(col * 128, 128)],
-                    wbuf.at[col, pl.ds(first, count)],
-                    sem.at[slot, col],
-                )
-            )
-        copies.append(
-            pltpu.make_async_copy(down, wdown.at[pl.ds(first, count)], sem.at[slot, 16])
-        )
-        return copies
-
-    fresh = flags[0] == 1
-    low = pl.multiple_of(flags[1] * 176, 16)
-    high = pl.multiple_of(176 - flags[1] * 176, 16)
-
-    def both():
-        return fetch(a_gu, a_down, low, 176, 0) + fetch(b_gu, b_down, high, 176, 1)
-
-    def single():
-        return fetch(s_gu, s_down, 0, 352, 0)
-
-    @pl.when(fresh)
-    def _():
-        for copy in both():
-            copy.start()
-
-    @pl.when(jnp.logical_not(fresh))
-    def _():
-        for copy in single():
-            copy.start()
-
-    @pl.loop(0, 16)
-    def _(i):
-        span = pl.ds(pl.multiple_of(i * 64, 64), 64)
-        field = x[span, :].astype(F32)
-        inv = lax.rsqrt(jnp.mean(field * field, axis=-1, keepdims=True) + 1e-6)
-        xn[span, :] = (field * inv * gain[...]).astype(BF)
-
-    @pl.when(fresh)
-    def _():
-        for copy in both():
-            copy.wait()
-
-    @pl.when(jnp.logical_not(fresh))
-    def _():
-        for copy in single():
-            copy.wait()
-
-    flat = wbuf.reshape(16, 704, 128)
-    for first, count in ((0, 256), (256, 256), (512, 192)):
-        perm = split_matrix(count)
-        half = count // 2
-        for col in range(8):
-            pair = jnp.concatenate(
-                [flat[2 * col + i, first : first + count, :] for i in range(2)], axis=1
-            )
-            split = jnp.dot(perm, pair, preferred_element_type=F32).astype(BF)
-            for kind in range(2):
-                weights[kind, first // 2 : first // 2 + half, col * 256 : col * 256 + 256] = split[
-                    kind * half : kind * half + half
-                ]
-
-    @pl.loop(0, 8)
-    def _(i):
-        span = pl.ds(pl.multiple_of(i * 128, 128), 128)
-        block = xn[span, :]
-        gate = nt(block, weights[0])
-        up = nt(block, weights[1])
-        act = (gate / (1.0 + jnp.exp(-gate)) * up).astype(BF)
-        result = jnp.dot(act, wdown[...], preferred_element_type=F32).astype(BF)
-        for part in range(8):
-            y[part, span, :] = result[:, part * 256 : part * 256 + 256]
-
-
-def experts(flags, x, gain, *weights):
-    return pl.pallas_call(
-        experts_kernel,
-        out_shape=jax.ShapeDtypeStruct((8, 1024, 256), BF),
-        in_specs=[SMEM, VMEM, VMEM] + [ANY] * 6,
-        out_specs=VMEM,
-        scratch_shapes=[
-            pltpu.VMEM((16, 352, 2, 128), BF),
-            pltpu.VMEM((352, 2048), BF),
-            pltpu.VMEM((2, 352, 2048), BF),
-            pltpu.VMEM((1024, 2048), BF),
-            DMA((2, 17)),
-        ],
-        compiler_params=pltpu.CompilerParams(vmem_limit_bytes=48 << 20),
-        name="experts",
-    )(flags, x, gain, *weights)
-
-
-def return_kernel(y, back, tbuf, sums, lsem, a_s, a_r, b_s, b_r):
-    s, t = places()
-    z, r = s // 4, s % 4
-    far = [seq_peer(s, t, k, j) for k in range(8) for j in range(4) if (k, j) != (0, 0)]
-    greet(tp_peers(s, t) + far)
-    firsts, locals_ = [], []
-    for k in ORDER:
-        here = pl.ds(((z + k) % 8) * 4, 4)
-        for m in range(1, 8):
-            firsts.append(
-                push(y.at[t ^ m, here], tbuf.at[t, here], a_s.at[k, m], a_r.at[k, m], (s, t ^ m))
-            )
-        keep = pltpu.make_async_copy(y.at[t, here], tbuf.at[t, here], lsem.at[k])
-        keep.start()
-        locals_.append(keep)
-    seconds = []
-    last = None
-    for place, k in enumerate(ORDER):
-        group = ((z + k) % 8) * 4
-        here = pl.ds(group, 4)
-        for copy in firsts[place * 7 : place * 7 + 7]:
-            copy.wait_recv()
-        locals_[place].wait()
-        for par in range(2):
-            first = tbuf[par, here].astype(F32) + tbuf[par + 2, here].astype(F32)
-            second = tbuf[par + 4, here].astype(F32) + tbuf[par + 6, here].astype(F32)
-            sums[par, here] = (first + second).astype(BF)
-        for j in range(4):
-            target = group + (r ^ j)
-            if (k, j) == (0, 0):
-                last = pltpu.make_async_copy(sums.at[:, target], back.at[:, s], lsem.at[8])
-                last.start()
-            else:
-                seconds.append(
-                    push(sums.at[:, target], back.at[:, s], b_s.at[k, j], b_r.at[k, j], (target, t))
-                )
-    for copy in firsts:
-        copy.wait_send()
-    for copy in seconds:
-        copy.wait()
-    last.wait()
-
-
-def give_back(y):
-    return pl.pallas_call(
-        return_kernel,
-        out_shape=jax.ShapeDtypeStruct((2, 32, 32, 256), BF),
-        in_specs=[ANY],
-        out_specs=ANY,
-        scratch_shapes=[
-            pltpu.VMEM((8, 32, 32, 256), BF),
-            pltpu.VMEM((2, 32, 32, 256), BF),
-            DMA((9,)),
-            DMA((8, 8)),
-            DMA((8, 8)),
+            DMA((8, 2, 4)),
+            DMA((8, 2, 4)),
+            DMA((8, 4)),
+            DMA((8, 4)),
+            DMA((8,)),
+            DMA((8,)),
             DMA((8, 4)),
             DMA((8, 4)),
         ],
         compiler_params=pltpu.CompilerParams(
-            collective_id=3, has_side_effects=True, vmem_limit_bytes=24 << 20
+            collective_id=2, has_side_effects=True, vmem_limit_bytes=48 << 20
         ),
-        name="give_back",
-    )(y)
+        name="moe",
+    )(*operands)
 
 
 def combine_kernel(back, hidden, rank, routes, stats, out):
@@ -599,11 +737,15 @@
 ):
     t = lax.axis_index("tp")
     s = lax.axis_index("seq")
-    own_gu = fresh_gu[0].astype(BF)
-    own_down = fresh_down[0].astype(BF)
+    tok_all, w_all, own_gu, own_down, serve_gu = gather(
+        tokens,
+        qkv_train.transpose(1, 0, 2),
+        out_train,
+        fresh_gu[0],
+        fresh_down[0],
+        server_gu[0],
+    )
     other_gu, other_down = swapped((own_gu, own_down))
-    shard = jnp.concatenate([qkv_train.reshape(64, 768), out_train], axis=1).astype(BF)
-    tok_all, w_all = gather(tokens, shard)
 
     context = ctx_len[0]
     half = HEAD_DIM // 2
@@ -638,23 +780,21 @@
     gain_part = lax.dynamic_slice_in_dim(moe_gain, columns, 256, 0).reshape(1, 256)
     router_part = lax.dynamic_slice_in_dim(router, columns, 256, 0).T
     hidden, rows, stats = send_rows(got, tokens, rank, routes_t, router_part, gain_part)
-    x, stats_all = dispatch(rows.reshape(2, 32, 32, 256), stats)
-
     parity = t % 2
     use_fresh = lax.dynamic_index_in_dim(handed_half, s, 0, keepdims=False) == parity
-    flags = jnp.stack([use_fresh.astype(jnp.int32), parity.astype(jnp.int32)])
-    y = experts(
-        flags,
-        x.reshape(1024, 2048),
+    flag = jnp.broadcast_to(use_fresh.astype(F32), (1, 2048))
+    back, stats_all = moe(
+        rows.reshape(2, 32, 32, 256),
+        stats,
+        flag,
         moe_gain.reshape(1, 2048),
-        server_gu[0],
+        serve_gu,
         server_down[0],
         own_gu,
         own_down,
         other_gu,
         other_down,
     )
-    back = give_back(y.reshape(8, 32, 32, 256))
     return combine(back.reshape(8, 256, 256), hidden, rank, routes_t, stats_all)
 
 

time: 279 us -> 253 us (0.907)
  Pallas kernels: 259 us -> 226 us
  local copies, waits for them, and re-layouts: 8.63 us -> 22 us
  other arithmetic: 6.28 us -> 0.83 us
    pallas_call x3 -> x1, Pallas kernels: 171 us -> 128 us  [moe(): pl.pallas_call(moe_kernel, out_shape=(jax.ShapeDtypeStruct((2, 32, 32, 25...]
    pallas_call x1, Pallas kernels: 14.5 us -> 39.9 us  [scatter_sum(): pl.pallas_call(scatter_sum_kernel, out_shape=jax.ShapeDtypeStruct((8, 256...]
    pallas_call x1, Pallas kernels: 54.6 us -> 39.2 us  [gather(): pl.pallas_call(gather_kernel, out_shape=(jax.ShapeDtypeStruct((256, 2048)...]
    unnamed x26 -> x46, local copies, waits for them, and re-layouts: 6.77 us -> 20.1 us
    convert_element_type x2 -> x0, other arithmetic: 4.69 us -> none  [the longest x1 3.18 us: body(): own_gu = fresh_gu[0].astype(BF)]
  transfers between devices with their start and end apart: 2 -> 2, of which waited for: 0 -> 0; matrix products, arithmetic and copies ran while one was open for 3% -> 1% of each run, Pallas kernels for 57% -> 22%
where the time goes in v2:
time: 253 us
  Pallas kernels  226 us (89%)
  local copies, waits for them, and re-layouts  22 us (9%)
    pallas_call x1, Pallas kernels, moe(): pl.pallas_call(moe_kernel, out_shape=(jax.ShapeDtypeStruct((2, 32, 32, 25...  128 us
    pallas_call x1, Pallas kernels, scatter_sum(): pl.pallas_call(scatter_sum_kernel, out_shape=jax.ShapeDtypeStruct((8, 256...  39.9 us
    pallas_call x1, Pallas kernels, gather(): pl.pallas_call(gather_kernel, out_shape=(jax.ShapeDtypeStruct((256, 2048)...  39.2 us
    unnamed x46, local copies, waits for them, and re-layouts  20.1 us
    pallas_call x1, Pallas kernels, attention(): pl.pallas_call(attention_kernel, out_shape=jax.ShapeDtypeStruct((8, 256,...  13.3 us
  transfers between devices with their start and end apart: 2, of which 0 were waited for; matrix products, arithmetic and copies ran while one was open for 1% of the time, Pallas kernels for 22%

profile of v2, /device:TPU:1, one launch (start us, length us, event | category | flops | bytes accessed | tf_op | source)
XLA Modules:
  0.0 252.7 jit_solution(7420171107997648860)
XLA Ops:
  0.0 1.9 copy-done.5
  1.9 1.8 copy-done.6
  3.7 1.4 copy-done.10
  5.0 0.9 copy-done.13
  5.9 0.9 copy-done.14
  6.9 0.8 copy-done.16
  7.7 39.2 %gather_inputs.1 = (bf16[256,2048]{1,0:T(8,128)(2,1)S(1)}, bf16[8,2,2,64,1024]{4,3,2,1,0:T(8,128)(2,1)S(1)}, bf16[2,176,2048]{2,1,0:T(8,128)(2,1)S(1)}, bf16[176...) custom-call(bf16[256,256]{1,0:T(8,128)(2,1)S(1)} %copy-done.13, f32[3,64,256]{2,1,0:T(8,128)S(1)} %bitcast.28, ...), custom_call_target="tpu_custom_call" | custom-call | tf_op jit(solution)/shard_map/gather_inputs/pallas_call | solution.py:187
  47.0 1.9 copy-done.3
  48.9 1.6 copy-done.7
  50.5 0.4 collective-permute-start
  50.9 1.1 collective-permute-start.1
  52.7 0.5 fusion
  53.3 0.1 pad_maximum_fusion
  53.4 0.0 copy-start.2
  53.4 2.2 copy-done.2
  55.6 2.2 copy-done.4
  57.8 13.3 %attention.1.part = bf16[8,256,256]{2,1,0:T(8,128)(2,1)S(1)} custom-call(bf16[256,2048]{1,0:T(8,128)(2,1)S(1)} %get-tuple-element.15.tok, bf16[2048,1024]{1,0:T(8,128)(2,1)S(1)} %bitcast.21, f32[1,2048]{1,0:T(1,128)S(1)} %bitcast.30, f32[256,128]{1,0:T(8,128)S(1)} %get-tuple-element.28.cosf, f32[256,128]{1,0:T(8,128)S(1)} %get-tuple-element.29.sinf, ...), custom_call_target="tpu_custom_call" | custom-call | tf_op jit(solution)/shard_map/attention/pallas_call | solution.py:312
  71.1 0.9 copy-done.1
  72.0 39.9 %project_exchange.1.got = bf16[8,256,256]{2,1,0:T(8,128)(2,1)} custom-call(bf16[8,256,256]{2,1,0:T(8,128)(2,1)} %copy-done.1), custom_call_target="tpu_custom_call" | custom-call | tf_op jit(solution)/shard_map/project_exchange/pallas_call | solution.py:344
  111.9 0.6 dynamic_slice.12
  113.2 0.7 dynamic_slice.11
  113.9 0.6 dynamic-slice_bitcast_fusion.router
  114.5 0.1 compare_reduce_fusion
  114.6 0.8 convolution_select_fusion.rank
  115.4 2.8 %send_rows.1 = (bf16[256,256]{1,0:T(8,128)(2,1)}, bf16[8,256,256]{2,1,0:T(8,128)(2,1)}, f32[8,256]{1,0:T(8,128)}) custom-call(bf16[8,256,256]{2,1,0:T(8,128)(2,1)} %project_exchange.1.got, bf16[256,256]{1,0:T(8,128)(2,1)} %tok.3, f32[64,256]{1,0:T(8,128)} %convolution_select_fusion.rank, s32[6,256]{1,0:T(8,128)} %bitcast.31, ...), custom_call_target="tpu_custom_call" | custom-call | tf_op jit(solution)/shard_map/send_rows/pallas_call | solution.py:382
  118.2 0.0 collective-permute-done.1.b_down
  118.3 1.2 copy-done.12
  119.5 0.7 copy-done.19
  120.2 128.1 %moe.1 = (bf16[2,32,32,256]{3,2,1,0:T(8,128)(2,1)S(1)}, f32[8,8,256]{2,1,0:T(8,128)S(1)}) custom-call(bf16[2,32,32,256]{3,2,1,0:T(8,128)(2,1)S(1)} %bitcast.27, f32[8,256]{1,0:T(8,128)S(1)} %copy-done.19, f32[1,2048]{1,0:T(1,128)S(1)} %broadcast_in_dim.20.flag, f32[1,2048]{1,0:T(1,128)S(1)} %bitcast.29, bf16[2,352,2048]{2,1,0:T(8,128)(2,1)} %copy-done.7, ...), custom_call_target="tpu_custom_call" | custom-call | tf_op jit(solution)/shard_map/moe/pallas_call | solution.py:640
  248.3 1.0 copy-done.11
  249.3 0.6 copy-done.15
  249.9 2.8 %combine.1 = bf16[256,256]{1,0:T(8,128)(2,1)} custom-call(bf16[8,256,256]{2,1,0:T(8,128)(2,1)} %bitcast.26, bf16[256,256]{1,0:T(8,128)(2,1)} %get-tuple-element.23.hidden, f32[64,256]{1,0:T(8,128)} %convolution_select_fusion.rank, s32[6,256]{1,0:T(8,128)} %bitcast.32, f32[8,8,256]{2,1,0:T(8,128)} %copy-done.15), custom_call_target="tpu_custom_call" | custom-call | tf_op jit(solution)/shard_map/combine/pallas_call | solution.py:708
  (36 shorter events, 0.1 us)
Async XLA Ops:
  0.0 113.9 %copy-start = (bf16[2048,64]{0,1:T(8,128)(2,1)S(1)}, bf16[2048,64]{0,1:T(8,128)(2,1)}, u32[]{:S(2)}) copy-start(bf16[2048,64]{0,1:T(8,128)(2,1)} %param.23) | copy-start | bytes 786436
  0.0 1.9 copy-start.5
  1.9 1.8 copy-start.6
  3.7 1.4 copy-start.10
  5.0 0.9 copy-start.13
  5.9 0.9 copy-start.14
  6.9 0.8 copy-start.16
  7.7 45.0 %copy-start.21 = (s32[1,4096]{1,0:T(1,128)S(1)}, s32[1,4096]{1,0:T(1,128)}, u32[]{:S(2)}) copy-start(s32[1,4096]{1,0:T(1,128)} %param.18) | copy-start | bytes 49156
  7.7 45.7 %copy-start.18 = (f32[2048]{0:T(1024)S(1)}, f32[2048]{0:T(1024)}, u32[]{:S(2)}) copy-start(f32[2048]{0:T(1024)} %param.19) | copy-start | bytes 24580
  47.0 2.0 copy-start.3
  48.9 1.6 copy-start.7
  50.5 20.6 %copy-start.9 = (bf16[2,176,2048]{2,1,0:T(8,128)(2,1)}, bf16[2,176,2048]{2,1,0:T(8,128)(2,1)S(1)}, u32[]{:S(2)}) copy-start(bf16[2,176,2048]{2,1,0:T(8,128)(2,1)S(1)} %get-tuple-element.20.a_gu) | copy-start | bytes 4325380
  50.5 67.7 %collective-permute-start = (bf16[2,176,2048]{2,1,0:T(8,128)(2,1)S(1)}, bf16[2,176,2048]{2,1,0:T(8,128)(2,1)}, u32[]{:S(2)}, u32[]{:S(2)}) collective-permute-start(bf16[2,176,2048]{2,1,0:T(8,128)(2,1)S(1)} %get-tuple-element.20.a_gu), channel_id=1, source_target_pairs={{0,1},{1,0},{2,3},{3,2},{4,5},{5,4},{6,7},{7,6},{8,9},{9,8},{10,11... | collective-permute-start | bytes 4325384 | tf_op jit(solution)/shard_map/ppermute | solution.py:718
  50.9 67.3 %collective-permute-start.1 = (bf16[176,2048]{1,0:T(8,128)(2,1)}, bf16[176,2048]{1,0:T(8,128)(2,1)}, u32[]{:S(2)}, u32[]{:S(2)}) collective-permute-start(bf16[176,2048]{1,0:T(8,128)(2,1)} %get-tuple-element.21.a_down), channel_id=1, source_target_pairs={{0,1},{1,0},{2,3},{3,2},{4,5},{5,4},{6,7},{7,6},{8,9},{9,8},{10,11... | collective-permute-start | bytes 2162696 | tf_op jit(solution)/shard_map/ppermute | solution.py:718
  53.4 2.2 copy-start.2
  55.6 2.2 copy-start.4
  57.8 54.1 %copy-start.22 = (s32[32]{0:T(128)S(1)}, s32[32]{0:T(128)}, u32[]{:S(2)}) copy-start(s32[32]{0:T(128)} %param.25) | copy-start | bytes 388
  57.8 55.4 %copy-start.17 = (f32[2048]{0:T(1024)S(1)}, f32[2048]{0:T(1024)}, u32[]{:S(2)}) copy-start(f32[2048]{0:T(1024)} %param.20) | copy-start | bytes 24580
  57.8 56.7 %copy-start.20 = (s32[256,6]{0,1:T(8,128)S(1)}, s32[256,6]{0,1:T(8,128)}, u32[]{:S(2)}) copy-start(s32[256,6]{0,1:T(8,128)} %param.24) | copy-start | bytes 18436
  71.1 0.9 copy-start.1
  72.0 46.2 %copy-start.8 = (bf16[1,352,2048]{2,1,0:T(8,128)(2,1)S(1)}, bf16[1,352,2048]{2,1,0:T(8,128)(2,1)}, u32[]{:S(2)}) copy-start(bf16[1,352,2048]{2,1,0:T(8,128)(2,1)} %param.29) | copy-start | bytes 4325380
  118.3 1.2 copy-start.12
  119.5 0.7 copy-start.19
  248.3 1.0 copy-start.11
  249.3 0.6 copy-start.15

commit v3 on v0

v3 whole, which is shorter than its diff:
```python
import functools

import jax
import jax.numpy as jnp
from jax import lax
from jax.experimental import pallas as pl
from jax.experimental.pallas import tpu as pltpu
from jax.sharding import PartitionSpec as P

HEAD_DIM = 128
SINK = 4
WIN = 4096
MESH = pl.DeviceIdType.MESH
BF = jnp.bfloat16
F32 = jnp.float32
ANY = pl.BlockSpec(memory_space=pl.ANY)
VMEM = pl.BlockSpec(memory_space=pltpu.VMEM)
SMEM = pl.BlockSpec(memory_space=pltpu.SMEM)
DMA = pltpu.SemaphoreType.DMA


def places():
    return lax.axis_index("seq"), lax.axis_index("tp")


def greet(peers):
    barrier = pltpu.get_barrier_semaphore()
    for peer in peers:
        pl.semaphore_signal(barrier, inc=1, device_id=peer, device_id_type=MESH)
    pl.semaphore_wait(barrier, len(peers))


def remote(src, dst, send, recv, peer):
    return pltpu.make_async_remote_copy(
        src_ref=src, dst_ref=dst, send_sem=send, recv_sem=recv, device_id=peer, device_id_type=MESH
    )


def push(src, dst, send, recv, peer):
    copy = remote(src, dst, send, recv, peer)
    copy.start()
    return copy


def tp_peers(s, t):
    return [(s, t ^ k) for k in range(1, 8)]


def seq_peer(s, t, k, j):
    z, r = s // 4, s % 4
    return ((z + k) % 8) * 4 + (r ^ j), t


def split_matrix(n):
    row = lax.broadcasted_iota(jnp.int32, (n, n), 0)
    col = lax.broadcasted_iota(jnp.int32, (n, n), 1)
    half = n // 2
    return jnp.where(col == jnp.where(row < half, 2 * row, 2 * (row - half) + 1), 1.0, 0.0).astype(BF)


def nt(a, b):
    return lax.dot_general(a, b, (((1,), (1,)), ((), ())), preferred_element_type=F32)


def slot_rows(rank, first):
    shelf = lax.broadcasted_iota(jnp.int32, (32, 256), 0).astype(F32)
    return [jnp.where(rank[first + e : first + e + 1, :] == shelf, 1.0, 0.0) for e in range(8)]


CHUNKS, WIDTH = 8, 512


def layer_kernel(
    tok,
    context,
    handed,
    qkv,
    proj,
    f_gu,
    f_down,
    s_gu,
    s_down,
    gain,
    moe_gain,
    cosine,
    sine,
    slots,
    cache,
    routes,
    router,
    out,
    hidden,
    rows,
    stats,
    s_gu_out,
    f_gu_out,
    f_down_out,
    o_gu_out,
    o_down_out,
    rank,
    share,
    final,
    wq,
    wo,
    wq_all,
    wo_all,
    tok_all,
    part,
    got,
    qbuf,
    pbuf,
    fbuf,
    sbuf,
    cbuf,
    scores,
    top,
    total,
    acc,
    xn,
    back,
    stats_all,
    stage,
    xstage,
    x,
    y,
    ybuf,
    halves,
    xbuf,
    sums,
    w_down,
    lsem,
    fsem,
    ssem,
    csem,
    tok_s,
    tok_r,
    swap_s,
    swap_r,
    x_s,
    x_r,
    z_s,
    z_r,
    c_s,
    c_r,
    p_s,
    p_r,
    g_s,
    g_r,
    d_s,
    d_r,
    dx_s,
    dx_r,
    dy_s,
    dy_r,
    ry_s,
    ry_r,
    rx_s,
    rx_r,
    r_s,
    r_r,
):
    s, t = places()
    z, xh, c = s // 4, (s // 2) % 2, s % 2
    up = (((z + 1) % 8) * 4 + xh * 2 + c, t)
    down = (((z + 7) % 8) * 4 + xh * 2 + c, t)
    over = (s ^ 2, t)
    twin = (s ^ 1, t)

    pull_q = pltpu.make_async_copy(qkv, qbuf, lsem.at[0])
    pull_p = pltpu.make_async_copy(proj, pbuf, lsem.at[1])
    pull_d = [
        pltpu.make_async_copy(
            f_down.at[:, pl.ds(i * 512, 512)], scores.at[0, i, pl.ds(0, 176)], lsem.at[10 + i]
        )
        for i in range(4)
    ]
    pull_w = pltpu.make_async_copy(s_down, w_down, lsem.at[6])
    pull_q.start()
    pull_p.start()
    for pull in pull_d:
        pull.start()
    f_pulls, s_pulls = [], []
    for col in range(16):
        span = pl.ds(col * 128, 128)
        f_pulls.append(pltpu.make_async_copy(f_gu.at[:, :, span], fbuf.at[col], fsem.at[col]))
        s_pulls.append(pltpu.make_async_copy(s_gu.at[:, :, span], sbuf.at[col], ssem.at[col]))
    for pull in f_pulls:
        pull.start()

    def fetch(i, h):
        span = pl.ds(pl.multiple_of(i * WIDTH, WIDTH), WIDTH)
        return pltpu.make_async_copy(
            cache.at[span, :, pl.ds(h * 128, 128)], cbuf.at[h, span], csem.at[i, h]
        )

    far = [seq_peer(s, t, k, j) for k in range(8) for j in range(4) if (k, j) != (0, 0)]
    greet(tp_peers(s, t) + far)
    spot = tok_all.at[:, pl.ds(pl.multiple_of(t * 256, 256), 256)]
    toks = [push(tok, spot, tok_s.at[k], tok_r.at[k], (s, t ^ k)) for k in range(1, 8)]
    local_t = pltpu.make_async_copy(tok, spot, lsem.at[3])
    local_t.start()
    pull_q.wait()
    for j in range(3):
        wq[:, j * 256 : j * 256 + 256] = qbuf[j].astype(BF)

    class Ring:
        def __init__(self, own, whole, which):
            self.own, self.whole, self.which = own, whole, which
            self.ups, self.downs, self.twins = {}, {}, []

        def block(self, dz, a):
            return self.whole.at[(z + dz + 8) % 8, xh ^ a, c]

        def pass_on(self, src, dst, step, a, ways):
            for way, chain, peer in ((0, self.ups, up), (1, self.downs, down)):
                if way in ways:
                    at = (self.which, way, step, a)
                    chain[(step, a)] = push(src, dst, z_s.at[at], z_r.at[at], peer)

        def to_twin(self, src, dst, place, a):
            at = (self.which, place, a)
            self.twins.append(push(src, dst, c_s.at[at], c_r.at[at], twin))

        def begin(self):
            home = self.block(0, 0)
            self.across = push(self.own, home, x_s.at[self.which], x_r.at[self.which], over)
            self.pass_on(self.own, home, 0, 0, (0, 1))
            self.to_twin(self.own, home, 0, 0)
            self.local = pltpu.make_async_copy(self.own, home, lsem.at[4 + self.which])
            self.local.start()

        def partner(self):
            self.across.wait_recv()
            theirs = self.block(0, 1)
            self.pass_on(theirs, theirs, 0, 1, (0, 1))
            self.to_twin(theirs, theirs, 0, 1)

        def turn(self, step, a, way):
            chain = (self.ups, self.downs)[way]
            if (step, a) not in chain:
                return
            chain[(step, a)].wait_recv()
            dz = (-1 - step, 1 + step)[way]
            here = self.block(dz, a)
            if step < 2 or (step == 2 and a == way):
                self.pass_on(here, here, step + 1, a, (way,))
            self.to_twin(here, here, dz % 8, a)

        def step(self, step):
            for a in range(2):
                for way in range(2):
                    self.turn(step, a, way)

        def arrive(self):
            for copy in self.twins:
                copy.wait_recv()
            self.local.wait()

        def end(self):
            self.across.wait_send()
            for copy in self.twins + list(self.ups.values()) + list(self.downs.values()):
                copy.wait_send()

    ring_q = Ring(wq.at[:, :], wq_all, 0)
    ring_o = Ring(wo.at[:, :], wo_all, 1)
    ring_q.begin()

    f_flat = fbuf.reshape(16, 352, 128)
    s_flat = sbuf.reshape(16, 704, 128)
    c_flat = [cbuf.at[h].reshape(8192, 128) for h in range(2)]
    keys, vals = y.at[0].reshape(4096, 256), y.at[1].reshape(4096, 256)
    swaps = []

    def swap(src, dst):
        i = len(swaps)
        swaps.append(push(src, dst, swap_s.at[i], swap_r.at[i], (s, t ^ 1)))

    def part_fresh():
        for col in range(16):
            f_pulls[col].wait()
            for kind in range(2):
                f_gu_out[kind, :, col * 128 : col * 128 + 128] = f_flat[
                    col, pl.ds(kind, 176, stride=2), :
                ].astype(BF)
        for kind in range(2):
            swap(f_gu_out.at[kind], o_gu_out.at[kind])
        for i in range(CHUNKS):
            for h in range(2):
                fetch(i, h).start()

    def part_down():
        for i in range(4):
            pull_d[i].wait()
            f_down_out[:, i * 512 : i * 512 + 512] = scores[0, i, 0:176].astype(BF)
        for pull in s_pulls:
            pull.start()
        pull_w.start()
        pull_p.wait()
        wo[...] = pbuf[...].astype(BF)

    def part_cache(i):
        for h in range(2):
            fetch(i, h).wait()
        perm = split_matrix(256)
        for k in range(4):
            start = i * 1024 + k * 256
            both = jnp.concatenate([c_flat[h][start : start + 256, :] for h in range(2)], axis=1)
            split = jnp.dot(perm, both, preferred_element_type=F32).astype(BF)
            spot = i * WIDTH + k * 128
            keys[spot : spot + 128, :] = split[0:128]
            vals[spot : spot + 128, :] = split[128:256]

    def part_server(col):
        for pull in s_pulls[2 * col : 2 + 2 * col]:
            pull.wait()
        for first, count in ((0, 256), (256, 256), (512, 192)):
            half = count // 2
            pair = jnp.concatenate(
                [s_flat[2 * col + i, first : first + count, :] for i in range(2)], axis=1
            )
            split = jnp.dot(split_matrix(count), pair, preferred_element_type=F32).astype(BF)
            for kind in range(2):
                s_gu_out[kind, first // 2 : first // 2 + half, col * 256 : col * 256 + 256] = split[
                    kind * half : kind * half + half
                ]

    def part_norm():
        for copy in toks:
            copy.wait_recv()
        local_t.wait()
        field = tok_all[...].astype(F32)
        inv = lax.rsqrt(jnp.mean(field * field, axis=-1, keepdims=True) + 1e-6)
        xn[...] = (field * inv * gain[...]).astype(BF)

    def part_rank():
        shelf = lax.broadcasted_iota(jnp.int32, (64, 256), 0)
        named = (shelf % 32) * 2 + shelf // 32
        hit = jnp.zeros((64, 256), F32)
        for k in range(6):
            hit += jnp.where(routes[k : k + 1, :] == named, 1.0, 0.0)
        row = lax.broadcasted_iota(jnp.int32, (256, 256), 0)
        col = lax.broadcasted_iota(jnp.int32, (256, 256), 1)
        later = jnp.where(row < col, 1.0, 0.0).astype(BF)
        before = jnp.dot(hit.astype(BF), later, preferred_element_type=F32)
        rank[...] = jnp.where(hit > 0.0, before, -1.0)

    work = [functools.partial(part_cache, i) for i in range(8)] + [part_rank]
    work += [functools.partial(part_server, col) for col in range(2)]
    work += [part_norm]
    work += [functools.partial(part_server, col) for col in range(2, 8)]
    part_fresh()
    ring_q.partner()
    part_down()
    for step in range(4):
        for a in range(2):
            for way in range(2):
                ring_q.turn(step, a, way)
                if work:
                    work.pop(0)()
    ring_o.begin()
    for piece in work:
        piece()
    ring_o.partner()
    ring_q.arrive()

    projected = jnp.dot(xn[...], wq_all[...].reshape(2048, 768), preferred_element_type=F32)
    ring_o.step(0)

    cosf = jnp.concatenate([cosine[...], cosine[...]], axis=1)
    sinf = jnp.concatenate([-sine[...], sine[...]], axis=1)

    def turned(field):
        return (field * cosf + pltpu.roll(field, 64, 1) * sinf).astype(BF)

    queries = [turned(projected[:, h * 128 : h * 128 + 128]) for h in range(2)]
    keys_new = [turned(projected[:, 256 + h * 128 : 384 + h * 128]) for h in range(2)]
    values_new = [projected[:, 512 + h * 128 : 640 + h * 128].astype(BF) for h in range(2)]
    row_id = lax.broadcasted_iota(jnp.int32, (256, WIDTH), 0)
    new_row = lax.broadcasted_iota(jnp.int32, (256, 256), 0)
    new_col = lax.broadcasted_iota(jnp.int32, (256, 256), 1)
    for h in range(2):
        fresh = jnp.where(new_col <= new_row, nt(queries[h], keys_new[h]), -1e30)
        scores[h, CHUNKS, :, 0:256] = fresh
        top[h] = jnp.maximum(fresh[:, 0:128], fresh[:, 128:256])

    def score(first, last):
        @pl.loop(first, last)
        def _(i):
            span = pl.ds(pl.multiple_of(i * WIDTH, WIDTH), WIDTH)
            slot = slots[:, span]
            limit = jnp.where(slot < 0, 0, jnp.where(slot < SINK, 256, slot + WIN - context[0]))
            seen = row_id < limit
            for h in range(2):
                block = nt(queries[h], keys[span, h * 128 : h * 128 + 128])
                block = jnp.where(seen, block, -1e30)
                scores[h, i] = block
                peak = jnp.maximum(
                    jnp.maximum(block[:, 0:128], block[:, 128:256]),
                    jnp.maximum(block[:, 256:384], block[:, 384:512]),
                )
                top[h] = jnp.maximum(top[h], peak)

    score(0, 4)
    ring_o.step(1)
    score(4, 8)
    ring_o.step(2)

    scale = 1.4426950408889634 / (HEAD_DIM**0.5)
    for h in range(2):
        top[h] = jnp.broadcast_to(jnp.max(top[h], axis=1, keepdims=True), (256, 128))
        peak = top[h]
        weights = jnp.exp2((scores[h, CHUNKS, :, 0:256] - jnp.tile(peak, (1, 2))) * scale)
        total[h] = weights[:, 0:128] + weights[:, 128:256]
        acc[h] = jnp.dot(weights.astype(BF), values_new[h], preferred_element_type=F32)

    def weigh(first, last):
        @pl.loop(first, last)
        def _(i):
            for h in range(2):
                weights = jnp.exp2((scores[h, i] - jnp.tile(top[h], (1, 4))) * scale)
                total[h] += (weights[:, 0:128] + weights[:, 128:256]) + (
                    weights[:, 256:384] + weights[:, 384:512]
                )
                span = pl.ds(pl.multiple_of(i * WIDTH, WIDTH), WIDTH)
                acc[h] += jnp.dot(
                    weights.astype(BF), vals[span, h * 128 : h * 128 + 128], preferred_element_type=F32
                )

    weigh(0, 4)
    ring_o.step(3)
    weigh(4, 8)
    ring_o.arrive()
    mixed = jnp.concatenate(
        [(acc[h] / jnp.sum(total[h], axis=1, keepdims=True)).astype(BF) for h in range(2)], axis=1
    )

    gives = []
    for k in (2, 6, 1, 3, 4, 5, 7, 0):
        part[k] = nt(mixed, wo_all[t ^ k].reshape(256, 256)).astype(BF)
        if k:
            gives.append(push(part.at[k], got.at[k], p_s.at[k], p_r.at[k], (s, t ^ k)))
    swap(f_down_out, o_down_out)
    for copy in gives:
        copy.wait_recv()
    total_out = tok[...].astype(F32) + part[0].astype(F32)
    for k in range(1, 8):
        total_out += got[k].astype(F32)
    state = total_out.astype(BF)
    hidden[...] = state
    for chunk in range(8):
        pick = jnp.concatenate(slot_rows(rank, chunk * 8), axis=0).astype(BF)
        picked = jnp.dot(pick, state, preferred_element_type=F32).astype(BF)
        first = (chunk % 4) * 8
        rows[chunk // 4, first : first + 8] = picked.reshape(8, 32, 256)
    side, mine = t // 4, t % 2
    cross = (s, t ^ 4)
    r = s % 4
    def distance(i):
        return jnp.where(i % 2 == 1, (i + 1) // 2, (8 - i // 2) % 8)

    def arriving(i, j):
        source = ((z + 8 - distance(i)) % 8) * 4 + (r ^ j)
        return remote(rows.at[:, source], stage.at[:, source], d_s.at[i, j], d_r.at[i, j], (s, t ^ 1))

    def leaving(i, j):
        target = ((z + distance(i)) % 8) * 4 + (r ^ j)
        return remote(rows.at[:, target], stage.at[:, s], d_s.at[i, j], d_r.at[i, j], (target, t))

    def group(i):
        return pl.ds(((z + 8 - distance(i)) % 8) * 4, 4)

    def crossing(i):
        here = group(i)
        return remote(stage.at[:, here], xstage.at[:, here], dx_s.at[i], dx_r.at[i], cross)

    def columns(which):
        owner = t ^ (4 * which)
        return pl.ds(pl.multiple_of(owner * 256, 256), 256)

    def spreading(i, which, m):
        here = group(i)
        buf = (stage, xstage)[which]
        return remote(
            buf.at[(t ^ m) % 2, here],
            x.at[here, :, columns(which)],
            dy_s.at[i, which, m],
            dy_r.at[i, which, m],
            (s, t ^ m),
        )

    def keeping(i, which):
        here = group(i)
        buf = (stage, xstage)[which]
        return pltpu.make_async_copy(
            buf.at[mine, here], x.at[here, :, columns(which)], dy_s.at[i, which, 0]
        )

    def sharing(i, m):
        here = group(i)
        return remote(
            y.at[:, (t ^ m) % 4, here], ybuf.at[m - 1, :, here], ry_s.at[i, m], ry_r.at[i, m], (s, t ^ m)
        )

    def joining(i):
        here = group(i)
        return remote(halves.at[1 - side, :, here], xbuf.at[:, here], rx_s.at[i], rx_r.at[i], cross)

    def returning(i, j):
        target = ((z + 8 - distance(i)) % 8) * 4 + (r ^ j)
        return remote(sums.at[:, target], back.at[:, s], r_s.at[i, j], r_r.at[i, j], (target, t))

    own_in = pltpu.make_async_copy(rows.at[:, s], stage.at[:, s], lsem.at[7])
    own_out = pltpu.make_async_copy(sums.at[:, s], back.at[:, s], lsem.at[8])
    own_in.start()
    for j in range(1, 4):
        leaving(0, j).start()

    @pl.loop(1, 8)
    def _(i):
        for j in range(4):
            leaving(i, j).start()

    def statistics(k):
        return remote(stats, stats_all.at[t], g_s.at[k], g_r.at[k], (s, t ^ k))

    span = pl.ds(pl.multiple_of(t * 256, 256), 256)
    wide = state.astype(F32)
    logits = nt(router[:, span], (wide * moe_gain[:, span]).astype(BF))
    expert = lax.broadcasted_iota(jnp.int32, (64, 256), 0)
    lines = [
        jnp.sum(jnp.where(routes[k : k + 1, :] == expert, logits, 0.0), axis=0, keepdims=True)
        for k in range(6)
    ]
    square = jnp.sum(jnp.transpose(wide * wide), axis=0, keepdims=True)
    stats[...] = jnp.concatenate(lines + [square, jnp.zeros((1, 256), F32)], axis=0)
    near = pltpu.make_async_copy(stats, stats_all.at[t], lsem.at[9])
    near.start()
    for k in range(1, 8):
        statistics(k).start()

    def choose():
        for copy in swaps:
            copy.wait_recv()
        pull_w.wait()
        chosen = jnp.broadcast_to(handed[s], (16, 2048)) == mine
        for first, gu, down in (
            (mine * 176, f_gu_out, f_down_out),
            (176 - mine * 176, o_gu_out, o_down_out),
        ):

            @pl.loop(0, 11)
            def _(i):
                here = pl.ds(pl.multiple_of(i * 16, 16), 16)
                there = pl.ds(pl.multiple_of(first + i * 16, 16), 16)
                for kind in range(2):
                    s_gu_out[kind, there, :] = jnp.where(
                        chosen, gu[kind, here, :].astype(F32), s_gu_out[kind, there, :].astype(F32)
                    ).astype(BF)
                w_down[there, :] = jnp.where(
                    chosen, down[here, :].astype(F32), w_down[there, :].astype(F32)
                ).astype(BF)

    def gates():
        near.wait()
        for k in range(1, 8):
            statistics(k).wait_recv()
        sums_of = stats_all[0]
        for k in range(1, 8):
            sums_of += stats_all[k]
        inv = lax.rsqrt(sums_of[6:7, :] * (1.0 / 2048.0) + 1e-6)
        gate = 1.0 / (1.0 + jnp.exp(-(sums_of * inv)))
        shelf = lax.broadcasted_iota(jnp.int32, (64, 256), 0)
        named = (shelf % 32) * 2 + shelf // 32
        amount = jnp.zeros((64, 256), F32)
        for k in range(6):
            amount += jnp.where(routes[k : k + 1, :] == named, gate[k : k + 1, :], 0.0)
        share[...] = amount
        final[...] = hidden[...].astype(F32)

    def arrive(i):
        @pl.when(i == 0)
        def _():
            own_in.wait()

        @pl.when(i > 0)
        def _():
            arriving(i, 0).wait_recv()

        for j in range(1, 4):
            arriving(i, j).wait_recv()
        crossing(i).start()
        for m in range(1, 4):
            spreading(i, 0, m).start()
        keeping(i, 0).start()

    def spread(i):
        crossing(i).wait_recv()
        for m in range(1, 4):
            spreading(i, 1, m).start()
        keeping(i, 1).start()

    def compute(i):
        for which in range(2):
            for m in range(1, 4):
                spreading(i, which, m).wait_recv()
            keeping(i, which).wait()
        here = group(i)
        field = x[here].reshape(128, 2048).astype(F32)
        inv = lax.rsqrt(jnp.mean(field * field, axis=-1, keepdims=True) + 1e-6)
        block = (field * inv * moe_gain[...]).astype(BF)
        gate = nt(block, s_gu_out[0])
        lift = nt(block, s_gu_out[1])
        act = (gate / (1.0 + jnp.exp(-gate)) * lift).astype(BF)
        for part in range(8):
            result = jnp.dot(
                act, w_down[:, part * 256 : part * 256 + 256], preferred_element_type=F32
            )
            y[part // 4, part % 4, here] = result.astype(BF).reshape(4, 32, 256)
        for m in range(1, 4):
            sharing(i, m).start()

    def fold(i):
        here = group(i)
        for m in range(1, 4):
            sharing(i, m).wait_recv()
        for col in range(2):
            same = y[col, t % 4, here].astype(F32) + ybuf[1, col, here].astype(F32)
            halves[col, mine, here] = same.astype(BF)
            other = ybuf[0, col, here].astype(F32) + ybuf[2, col, here].astype(F32)
            halves[col, 1 - mine, here] = other.astype(BF)
        joining(i).start()

    def finish(i):
        here = group(i)
        joining(i).wait_recv()
        for par in range(2):
            total = halves[side, par, here].astype(F32) + xbuf[par, here].astype(F32)
            sums[par, here] = total.astype(BF)

        @pl.when(i == 0)
        def _():
            own_out.start()

        @pl.when(i > 0)
        def _():
            returning(i, 0).start()

        for j in range(1, 4):
            returning(i, j).start()

    def collect(i):
        @pl.when(i == 0)
        def _():
            own_out.wait()

        @pl.when(i > 0)
        def _():
            returning(i, 0).wait_recv()

        for j in range(1, 4):
            returning(i, j).wait_recv()
        first = ((z + distance(i)) % 8) * 4
        shelf = lax.broadcasted_iota(jnp.int32, (32, 256), 0).astype(F32)
        for par in range(2):
            lines = []
            for e in range(4):
                line = pl.ds(par * 32 + first + e, 1)
                lines.append(jnp.where(rank[line, :] == shelf, share[line, :], 0.0))
            mix = jnp.concatenate(lines, axis=0)
            high = mix.astype(BF)
            low = (mix - high.astype(F32)).astype(BF)
            block = back[par, pl.ds(first, 4)].reshape(128, 256)
            dims = (((0,), (0,)), ((), ()))
            final[...] += lax.dot_general(
                high, block, dims, preferred_element_type=F32
            ) + lax.dot_general(low, block, dims, preferred_element_type=F32)

    @pl.loop(0, 14)
    def _(i):
        @pl.when(i == 2)
        def _():
            choose()

        @pl.when(i == 6)
        def _():
            gates()

        for lag, stage_of in ((0, arrive), (1, spread), (2, compute), (3, fold), (4, finish), (6, collect)):

            @pl.when((i >= lag) & (i < lag + 8))
            def _():
                stage_of(i - lag)

    out[...] = final[...].astype(BF)
    for k in range(1, 8):
        statistics(k).wait_send()
    for copy in swaps + gives + toks:
        copy.wait_send()
    ring_q.end()
    ring_o.end()

    def settle(i, j):
        leaving(i, j).wait_send()
        returning(i, j).wait_send()

    for j in range(1, 4):
        settle(0, j)

    @pl.loop(1, 8)
    def _(i):
        for j in range(4):
            settle(i, j)

    @pl.loop(0, 8)
    def _(i):
        crossing(i).wait_send()
        joining(i).wait_send()
        for m in range(1, 4):
            sharing(i, m).wait_send()
            for which in range(2):
                spreading(i, which, m).wait_send()


def layer(*operands):
    return pl.pallas_call(
        layer_kernel,
        out_shape=jax.ShapeDtypeStruct((256, 256), BF),
        in_specs=[VMEM, SMEM, SMEM] + [ANY] * 6 + [VMEM] * 5 + [ANY] + [VMEM] * 2,
        out_specs=VMEM,
        scratch_shapes=[
            pltpu.VMEM((256, 256), BF),
            pltpu.VMEM((2, 32, 32, 256), BF),
            pltpu.VMEM((8, 256), F32),
            pltpu.VMEM((2, 352, 2048), BF),
            pltpu.VMEM((2, 176, 2048), BF),
            pltpu.VMEM((176, 2048), BF),
            pltpu.VMEM((2, 176, 2048), BF),
            pltpu.VMEM((176, 2048), BF),
            pltpu.VMEM((64, 256), F32),
            pltpu.VMEM((64, 256), F32),
            pltpu.VMEM((256, 256), F32),
            pltpu.VMEM((64, 768), BF),
            pltpu.VMEM((64, 256), BF),
            pltpu.VMEM((8, 2, 2, 64, 768), BF),
            pltpu.VMEM((8, 2, 2, 64, 256), BF),
            pltpu.VMEM((256, 2048), BF),
            pltpu.VMEM((8, 256, 256), BF),
            pltpu.VMEM((8, 256, 256), BF),
            pltpu.VMEM((3, 64, 256), F32),
            pltpu.VMEM((64, 256), F32),
            pltpu.VMEM((16, 176, 2, 128), F32),
            pltpu.VMEM((16, 352, 2, 128), BF),
            pltpu.VMEM((2, 4096, 2, 128), BF),
            pltpu.VMEM((2, 9, 256, 512), F32),
            pltpu.VMEM((2, 256, 128), F32),
            pltpu.VMEM((2, 256, 128), F32),
            pltpu.VMEM((2, 256, 128), F32),
            pltpu.VMEM((256, 2048), BF),
            pltpu.VMEM((2, 32, 32, 256), BF),
            pltpu.VMEM((8, 8, 256), F32),
            pltpu.VMEM((2, 32, 32, 256), BF),
            pltpu.VMEM((2, 32, 32, 256), BF),
            pltpu.VMEM((32, 32, 2048), BF),
            pltpu.VMEM((2, 4, 32, 32, 256), BF),
            pltpu.VMEM((3, 2, 32, 32, 256), BF),
            pltpu.VMEM((2, 2, 32, 32, 256), BF),
            pltpu.VMEM((2, 32, 32, 256), BF),
            pltpu.VMEM((2, 32, 32, 256), BF),
            pltpu.VMEM((352, 2048), BF),
            DMA((14,)),
            DMA((16,)),
            DMA((16,)),
            DMA((8, 2)),
            DMA((8,)),
            DMA((8,)),
            DMA((3,)),
            DMA((3,)),
            DMA((2,)),
            DMA((2,)),
            DMA((2, 2, 4, 2)),
            DMA((2, 2, 4, 2)),
            DMA((2, 8, 2)),
            DMA((2, 8, 2)),
            DMA((8,)),
            DMA((8,)),
            DMA((8,)),
            DMA((8,)),
            DMA((8, 4)),
            DMA((8, 4)),
            DMA((8,)),
            DMA((8,)),
            DMA((8, 2, 4)),
            DMA((8, 2, 4)),
            DMA((8, 4)),
            DMA((8, 4)),
            DMA((8,)),
            DMA((8,)),
            DMA((8, 4)),
            DMA((8, 4)),
        ],
        compiler_params=pltpu.CompilerParams(
            collective_id=0, has_side_effects=True, vmem_limit_bytes=60 << 20
        ),
        name="layer",
    )(*operands)


def body(
    tokens,
    ctx_len,
    cache_kv,
    cache_pos,
    attn_gain,
    moe_gain,
    qkv_train,
    out_train,
    router,
    routes,
    handed_half,
    fresh_gu,
    fresh_down,
    server_gu,
    server_down,
):
    half = HEAD_DIM // 2
    frequency = 10000.0 ** (-jnp.arange(half, dtype=F32) / half)
    positions = ctx_len[0] + jnp.arange(256, dtype=jnp.int32)
    angles = positions.astype(F32)[:, None] * frequency[None, :]
    return layer(
        tokens,
        ctx_len,
        handed_half,
        qkv_train.transpose(1, 0, 2),
        out_train,
        fresh_gu[0],
        fresh_down[0],
        server_gu[0],
        server_down[0],
        attn_gain.reshape(1, 2048),
        moe_gain.reshape(1, 2048),
        jnp.cos(angles),
        jnp.sin(angles),
        cache_pos,
        cache_kv[0],
        routes.T,
        router.T,
    )


def solution(mesh):
    placed = (
        P("seq", "tp"),
        P("seq"),
        P("seq", None, None, "tp"),
        P("seq", None),
        P(),
        P(),
        P("seq", None, "tp"),
        P("seq", "tp"),
        P(),
        P("seq", None),
        P(),
        P("seq", "tp", None, None),
        P("seq", "tp", None),
        P("seq", "tp", None, None),
        P("seq", "tp", None),
    )
    return jax.shard_map(
        body, mesh=mesh, in_specs=placed, out_specs=P("seq", "tp"), check_vma=False
    )
```

time: 696 us -> 213 us (0.31)
  waiting for transfers between devices: 488 us -> 0 us
  Pallas kernels: 0 us -> 209 us
  local copies, waits for them, and re-layouts: 76.1 us -> 1.57 us
  other arithmetic: 60.2 us -> 1.25 us
  matrix products: 29.1 us -> 0 us
  starting transfers between devices: 27 us -> 0 us
  between operations: 14.8 us -> 0.67 us
    pallas_call x0 -> x1, Pallas kernels: none -> 209 us  [layer(): pl.pallas_call(layer_kernel, out_shape=jax.ShapeDtypeStruct((256, 256), B...]
    all_gather x3 -> x0, waiting for transfers between devices: 165 us -> none  [the longest x1 90.5 us: body(): lax.all_gather(qkv_train.astype(jnp.bfloat16), 'seq', axis=0, tiled=True)]
    all_to_all x2 -> x0, waiting for transfers between devices: 148 us -> none  [the longest x1 134 us: body(): lax.all_to_all(outgoing, 'seq', split_axis=0, concat_axis=0, tiled=True)]
    reduce_scatter x1 -> x0, waiting for transfers between devices: 90.4 us -> none  [body(): lax.psum_scatter(placed.astype(jnp.bfloat16), 'tp', scatter_dimension=3,...]
    psum x1 -> x0, waiting for transfers between devices: 53.8 us -> none  [body(): lax.psum(partial_out.astype(jnp.bfloat16), 'tp').astype(jnp.float32)]
    another operation x5 -> x0, other arithmetic: 34.6 us -> none
    ppermute x2 -> x0, waiting for transfers between devices: 30.2 us -> none  [swapped(): lax.ppermute(array, axis, [(i, i ^ 1 << apart) for i in range(lax.axis_si...]
    dot_general x7 -> x0, matrix products: 29.1 us -> none  [the longest x1 7.27 us: body(): jnp.einsum('sqcd,qfgd->sqcgf', mine, weights_gu, preferred_element_type=j...]
  transfers between devices with their start and end apart: 9 -> 0, of which waited for: 8 -> 0; matrix products, arithmetic and copies ran while one was open for 15% -> 0% of each run, Pallas kernels for 0% -> 0%
where the time goes in v3:
time: 213 us; the launch traced here: 212 us
  Pallas kernels  209 us (98%)
    pallas_call x1, Pallas kernels, layer(): pl.pallas_call(layer_kernel, out_shape=jax.ShapeDtypeStruct((256, 256), B...  209 us

profile of v3, /device:TPU:1, one launch (start us, length us, event | category | flops | bytes accessed | tf_op | source)
XLA Modules:
  0.0 212.4 jit_solution(17481650636208688839)
XLA Ops:
  0.7 1.2 multiply_sine_fusion
  1.9 208.9 %layer.1 = bf16[256,256]{1,0:T(8,128)(2,1)} custom-call(bf16[256,256]{1,0:T(8,128)(2,1)} %tok.1, s32[1]{0:T(128)} %copy.17.context, s32[32]{0:T(128)} %handed.1, f32[3,64,256]{2,1,0:T(8,128)} %bitcast.18, f32[64,256]{1,0:T(8,128)} %proj.1, f32[176,2,2048]{2,1,0:T(2,128)} %bitcast.13, f32[176,2048]{1,0:T(8,128)} %bitcast.15, bf16[352,2,2048]{2,1,0:T(2,128)(2,1)} %bitcast.14, ...), custom_call_target="tpu_custom_call" | custom-call | tf_op jit(solution)/shard_map/layer/pallas_call | solution.py:725
  210.9 1.6 copy.18
  (2 shorter events, 0.0 us)

commit v4 on v3

--- a/solution.py
+++ b/solution.py
@@ -456,7 +456,10 @@
     cross = (s, t ^ 4)
     r = s % 4
     def distance(i):
-        return jnp.where(i % 2 == 1, (i + 1) // 2, (8 - i // 2) % 8)
+        return jnp.where(i == 7, 0, jnp.where(i % 2 == 0, i // 2 + 1, 7 - i // 2))
+
+    def plain(i):
+        return (i != 2) & (i != 5)
 
     def arriving(i, j):
         source = ((z + 8 - distance(i)) % 8) * 4 + (r ^ j)
@@ -512,13 +515,14 @@
     own_in = pltpu.make_async_copy(rows.at[:, s], stage.at[:, s], lsem.at[7])
     own_out = pltpu.make_async_copy(sums.at[:, s], back.at[:, s], lsem.at[8])
     own_in.start()
-    for j in range(1, 4):
-        leaving(0, j).start()
-
-    @pl.loop(1, 8)
+
+    @pl.loop(0, 7)
     def _(i):
         for j in range(4):
             leaving(i, j).start()
+
+    for j in range(1, 4):
+        leaving(7, j).start()
 
     def statistics(k):
         return remote(stats, stats_all.at[t], g_s.at[k], g_r.at[k], (s, t ^ k))
@@ -577,33 +581,59 @@
         share[...] = amount
         final[...] = hidden[...].astype(F32)
 
+    def widening(i):
+        here = group(i)
+        half = x.at[here, :, pl.ds(pl.multiple_of(side * 1024, 1024), 1024)]
+        return remote(half, half, dx_s.at[i], dx_r.at[i], cross)
+
     def arrive(i):
-        @pl.when(i == 0)
+        @pl.when(i == 7)
         def _():
             own_in.wait()
 
-        @pl.when(i > 0)
+        @pl.when(i < 7)
         def _():
             arriving(i, 0).wait_recv()
 
         for j in range(1, 4):
             arriving(i, j).wait_recv()
-        crossing(i).start()
+
+        @pl.when(plain(i))
+        def _():
+            crossing(i).start()
+
         for m in range(1, 4):
             spreading(i, 0, m).start()
         keeping(i, 0).start()
 
     def spread(i):
-        crossing(i).wait_recv()
-        for m in range(1, 4):
-            spreading(i, 1, m).start()
-        keeping(i, 1).start()
+        @pl.when(plain(i))
+        def _():
+            crossing(i).wait_recv()
+            for m in range(1, 4):
+                spreading(i, 1, m).start()
+            keeping(i, 1).start()
+
+    def widen(i):
+        @pl.when(jnp.logical_not(plain(i)))
+        def _():
+            for m in range(1, 4):
+                spreading(i, 0, m).wait_recv()
+            keeping(i, 0).wait()
+            widening(i).start()
 
     def compute(i):
-        for which in range(2):
-            for m in range(1, 4):
-                spreading(i, which, m).wait_recv()
-            keeping(i, which).wait()
+        @pl.when(plain(i))
+        def _():
+            for which in range(2):
+                for m in range(1, 4):
+                    spreading(i, which, m).wait_recv()
+                keeping(i, which).wait()
+
+        @pl.when(jnp.logical_not(plain(i)))
+        def _():
+            widening(i).wait_recv()
+
         here = group(i)
         field = x[here].reshape(128, 2048).astype(F32)
         inv = lax.rsqrt(jnp.mean(field * field, axis=-1, keepdims=True) + 1e-6)
@@ -616,10 +646,53 @@
                 act, w_down[:, part * 256 : part * 256 + 256], preferred_element_type=F32
             )
             y[part // 4, part % 4, here] = result.astype(BF).reshape(4, 32, 256)
-        for m in range(1, 4):
-            sharing(i, m).start()
+
+        @pl.when(plain(i))
+        def _():
+            for m in range(1, 4):
+                sharing(i, m).start()
+
+        @pl.when(jnp.logical_not(plain(i)))
+        def _():
+            for pair in range(2):
+                leaning(i, pair).start()
+
+    def leaning(i, pair):
+        here = group(i)
+        send, recv = ((ry_s.at[i, 0], ry_r.at[i, 0]), (rx_s.at[i], rx_r.at[i]))[pair]
+        return remote(
+            y.at[1 - side, pl.ds(2 * pair, 2), here], ybuf.at[pair, :, here], send, recv, cross
+        )
+
+    def landing(i, m):
+        here = group(i)
+        return (ybuf.at[2, 0, here], ybuf.at[2, 1, here], xbuf.at[0, here])[m - 1]
+
+    def scattering(i, m):
+        here = group(i)
+        row = (t ^ m) % 4
+        return remote(
+            halves.at[row // 2, row % 2, here], landing(i, m), ry_s.at[i, m], ry_r.at[i, m], (s, t ^ m)
+        )
+
+    def lean(i):
+        @pl.when(jnp.logical_not(plain(i)))
+        def _():
+            here = group(i)
+            for pair in range(2):
+                leaning(i, pair).wait_recv()
+            for row in range(4):
+                both = y[side, row, here].astype(F32) + ybuf[row // 2, row % 2, here].astype(F32)
+                halves[row // 2, row % 2, here] = both.astype(BF)
+            for m in range(1, 4):
+                scattering(i, m).start()
 
     def fold(i):
+        @pl.when(plain(i))
+        def _():
+            fold_plain(i)
+
+    def fold_plain(i):
         here = group(i)
         for m in range(1, 4):
             sharing(i, m).wait_recv()
@@ -632,16 +705,29 @@
 
     def finish(i):
         here = group(i)
-        joining(i).wait_recv()
-        for par in range(2):
-            total = halves[side, par, here].astype(F32) + xbuf[par, here].astype(F32)
-            sums[par, here] = total.astype(BF)
-
-        @pl.when(i == 0)
+
+        @pl.when(plain(i))
+        def _():
+            joining(i).wait_recv()
+            for par in range(2):
+                both = halves[side, par, here].astype(F32) + xbuf[par, here].astype(F32)
+                sums[par, here] = both.astype(BF)
+
+        @pl.when(jnp.logical_not(plain(i)))
+        def _():
+            for m in range(1, 4):
+                scattering(i, m).wait_recv()
+            row = t % 4
+            same = halves[row // 2, row % 2, here].astype(F32) + ybuf[2, 1, here].astype(F32)
+            sums[mine, here] = same.astype(BF)
+            other = ybuf[2, 0, here].astype(F32) + xbuf[0, here].astype(F32)
+            sums[1 - mine, here] = other.astype(BF)
+
+        @pl.when(i == 7)
         def _():
             own_out.start()
 
-        @pl.when(i > 0)
+        @pl.when(i < 7)
         def _():
             returning(i, 0).start()
 
@@ -649,11 +735,11 @@
             returning(i, j).start()
 
     def collect(i):
-        @pl.when(i == 0)
+        @pl.when(i == 7)
         def _():
             own_out.wait()
 
-        @pl.when(i > 0)
+        @pl.when(i < 7)
         def _():
             returning(i, 0).wait_recv()
 
@@ -675,9 +761,9 @@
                 high, block, dims, preferred_element_type=F32
             ) + lax.dot_general(low, block, dims, preferred_element_type=F32)
 
-    @pl.loop(0, 14)
+    @pl.loop(0, 18)
     def _(i):
-        @pl.when(i == 2)
+        @pl.when(i == 3)
         def _():
             choose()
 
@@ -685,7 +771,16 @@
         def _():
             gates()
 
-        for lag, stage_of in ((0, arrive), (1, spread), (2, compute), (3, fold), (4, finish), (6, collect)):
+        for lag, stage_of in (
+            (0, arrive),
+            (1, spread),
+            (2, widen),
+            (3, compute),
+            (5, lean),
+            (5, fold),
+            (7, finish),
+            (10, collect),
+        ):
 
             @pl.when((i >= lag) & (i < lag + 8))
             def _():
@@ -704,21 +799,33 @@
         returning(i, j).wait_send()
 
     for j in range(1, 4):
-        settle(0, j)
-
-    @pl.loop(1, 8)
+        settle(7, j)
+
+    @pl.loop(0, 7)
     def _(i):
         for j in range(4):
             settle(i, j)
 
     @pl.loop(0, 8)
     def _(i):
-        crossing(i).wait_send()
-        joining(i).wait_send()
         for m in range(1, 4):
-            sharing(i, m).wait_send()
-            for which in range(2):
-                spreading(i, which, m).wait_send()
+            spreading(i, 0, m).wait_send()
+
+        @pl.when(plain(i))
+        def _():
+            crossing(i).wait_send()
+            joining(i).wait_send()
+            for m in range(1, 4):
+                sharing(i, m).wait_send()
+                spreading(i, 1, m).wait_send()
+
+        @pl.when(jnp.logical_not(plain(i)))
+        def _():
+            widening(i).wait_send()
+            for pair in range(2):
+                leaning(i, pair).wait_send()
+            for m in range(1, 4):
+                scattering(i, m).wait_send()
 
 
 def layer(*operands):

time: 213 us -> 202 us (0.948)
  Pallas kernels: 209 us -> 198 us
    pallas_call x1, Pallas kernels: 209 us -> 198 us  [layer(): pl.pallas_call(layer_kernel, out_shape=jax.ShapeDtypeStruct((256, 256), B...]
where the time goes in v4:
time: 202 us; the launch traced here: 201 us
  Pallas kernels  198 us (98%)
    pallas_call x1, Pallas kernels, layer(): pl.pallas_call(layer_kernel, out_shape=jax.ShapeDtypeStruct((256, 256), B...  198 us

profile of v4, /device:TPU:1, one launch (start us, length us, event | category | flops | bytes accessed | tf_op | source)
XLA Modules:
  0.0 201.1 jit_solution(521035233688181059)
XLA Ops:
  0.7 1.2 multiply_sine_fusion
  1.9 197.7 %layer.1 = bf16[256,256]{1,0:T(8,128)(2,1)} custom-call(bf16[256,256]{1,0:T(8,128)(2,1)} %tok.1, s32[1]{0:T(128)} %copy.17.context, s32[32]{0:T(128)} %handed.1, f32[3,64,256]{2,1,0:T(8,128)} %bitcast.18, f32[64,256]{1,0:T(8,128)} %proj.1, f32[176,2,2048]{2,1,0:T(2,128)} %bitcast.13, f32[176,2048]{1,0:T(8,128)} %bitcast.15, bf16[352,2,2048]{2,1,0:T(2,128)(2,1)} %bitcast.14, ...), custom_call_target="tpu_custom_call" | custom-call | tf_op jit(solution)/shard_map/layer/pallas_call | solution.py:832
  199.6 1.6 copy.18
  (2 shorter events, 0.0 us)

commit v5 on v4

--- a/solution.py
+++ b/solution.py
@@ -68,6 +68,7 @@
 
 
 CHUNKS, WIDTH = 8, 512
+TOKEN_ORDER = (4, 6, 2, 5, 7, 1, 3)
 
 
 def layer_kernel(
@@ -196,7 +197,12 @@
     far = [seq_peer(s, t, k, j) for k in range(8) for j in range(4) if (k, j) != (0, 0)]
     greet(tp_peers(s, t) + far)
     spot = tok_all.at[:, pl.ds(pl.multiple_of(t * 256, 256), 256)]
-    toks = [push(tok, spot, tok_s.at[k], tok_r.at[k], (s, t ^ k)) for k in range(1, 8)]
+    toks = []
+
+    def share_tokens(count):
+        for k in TOKEN_ORDER[len(toks) : len(toks) + count]:
+            toks.append(push(tok, spot, tok_s.at[k], tok_r.at[k], (s, t ^ k)))
+
     local_t = pltpu.make_async_copy(tok, spot, lsem.at[3])
     local_t.start()
     pull_q.wait()
@@ -282,8 +288,6 @@
                 f_gu_out[kind, :, col * 128 : col * 128 + 128] = f_flat[
                     col, pl.ds(kind, 176, stride=2), :
                 ].astype(BF)
-        for kind in range(2):
-            swap(f_gu_out.at[kind], o_gu_out.at[kind])
         for i in range(CHUNKS):
             for h in range(2):
                 fetch(i, h).start()
@@ -348,23 +352,35 @@
     work += [functools.partial(part_server, col) for col in range(2)]
     work += [part_norm]
     work += [functools.partial(part_server, col) for col in range(2, 8)]
+    ring_q.partner()
     part_fresh()
-    ring_q.partner()
     part_down()
+    event = 0
     for step in range(4):
         for a in range(2):
             for way in range(2):
+                if (step, a) not in (ring_q.ups, ring_q.downs)[way]:
+                    continue
                 ring_q.turn(step, a, way)
+                share_tokens(1)
+                if event in (7, 8):
+                    swap(f_gu_out.at[event - 7], o_gu_out.at[event - 7])
+                if event == 4:
+                    ring_o.begin()
+                if event == 7:
+                    ring_o.partner()
+                if event == 9:
+                    ring_o.step(0)
+                if event == 12:
+                    ring_o.step(1)
+                event += 1
                 if work:
                     work.pop(0)()
-    ring_o.begin()
     for piece in work:
         piece()
-    ring_o.partner()
     ring_q.arrive()
 
     projected = jnp.dot(xn[...], wq_all[...].reshape(2048, 768), preferred_element_type=F32)
-    ring_o.step(0)
 
     cosf = jnp.concatenate([cosine[...], cosine[...]], axis=1)
     sinf = jnp.concatenate([-sine[...], sine[...]], axis=1)
@@ -401,9 +417,8 @@
                 top[h] = jnp.maximum(top[h], peak)
 
     score(0, 4)
-    ring_o.step(1)
+    ring_o.step(2)
     score(4, 8)
-    ring_o.step(2)
 
     scale = 1.4426950408889634 / (HEAD_DIM**0.5)
     for h in range(2):
@@ -426,9 +441,8 @@
                     weights.astype(BF), vals[span, h * 128 : h * 128 + 128], preferred_element_type=F32
                 )
 
-    weigh(0, 4)
     ring_o.step(3)
-    weigh(4, 8)
+    weigh(0, 8)
     ring_o.arrive()
     mixed = jnp.concatenate(
         [(acc[h] / jnp.sum(total[h], axis=1, keepdims=True)).astype(BF) for h in range(2)], axis=1

time: 202 us -> 201 us (level)
  no operation moved by 1% of the time
where the time goes in v5:
time: 201 us
  Pallas kernels  198 us (99%)
    pallas_call x1, Pallas kernels, layer(): pl.pallas_call(layer_kernel, out_shape=jax.ShapeDtypeStruct((256, 256), B...  198 us

profile of v5, /device:TPU:1, one launch (start us, length us, event | category | flops | bytes accessed | tf_op | source)
XLA Modules:
  0.0 201.0 jit_solution(11435823573856786189)
XLA Ops:
  0.7 1.2 multiply_sine_fusion
  1.9 197.6 %layer.1 = bf16[256,256]{1,0:T(8,128)(2,1)} custom-call(bf16[256,256]{1,0:T(8,128)(2,1)} %tok.1, s32[1]{0:T(128)} %copy.17.context, s32[32]{0:T(128)} %handed.1, f32[3,64,256]{2,1,0:T(8,128)} %bitcast.18, f32[64,256]{1,0:T(8,128)} %proj.1, f32[176,2,2048]{2,1,0:T(2,128)} %bitcast.13, f32[176,2048]{1,0:T(8,128)} %bitcast.15, bf16[352,2,2048]{2,1,0:T(2,128)(2,1)} %bitcast.14, ...), custom_call_target="tpu_custom_call" | custom-call | tf_op jit(solution)/shard_map/layer/pallas_call | solution.py:846
  199.5 1.6 copy.18
  (2 shorter events, 0.0 us)
